TPU v7x, 32 devices: a whole 2x2x4 slice. The times are simulated.
32 devices in a mesh: dp: 8 (over z, y), sub: 4 (over x, core).
Axes of the slice: x: 2, y: 2, z: 4, core: 2. Of those that a mesh axis runs over, the one named last changes fastest.
Arguments:
- queries: bfloat16 [32, 64, 576], P('dp'), may hold values from -195 to 195
- own_cache: bfloat16 [32, 1024, 576], P('dp', 'sub'), may hold values from -8 to 8
- own_len: int32 [32, 4], P('dp', 'sub'), may hold values from 2 to 256
- host_cache: bfloat16 [8, 4, 8, 1024, 576], P('dp', 'sub'), may hold values from -8 to 8
- host_len: int32 [8, 4, 8], P('dp', 'sub'), may hold values from 2 to 1024
- page_plan: int32 [8, 4, 8], P('dp', 'sub'), may hold values from 0 to 3
- value_up: bfloat16 [64, 512, 128], P('sub'), may hold values from -0.25 to 0.25
Outputs:
- attended: bfloat16 [32, 64, 128], P('dp', 'sub')
All inputs are finite; a program needn't handle non-finite values.
Results may differ from a plain program's by a relative error of at most 0.008.
Values may be sent and summed in bfloat16 or wider, within the bound.
No kernel may reach another device: no remote copies, remote signals or barrier semaphores. Data moves between devices by JAX's collectives and lax.ppermute only.
A program may use at most 128 MiB of HBM per device.

v0:
```python
import functools

import jax
import jax.numpy as jnp
from jax import lax
from jax.experimental import pallas as pl
from jax.experimental.pallas import tpu as pltpu
from jax.sharding import PartitionSpec as P


DL = 512
LANES = 128
TILES = DL // LANES
PIECE = 32
PLAN_LANE = 96
score_scale = 192 ** (-0.5)
masked_score = -1e30


OWN_LIMIT = 42 << 20
PACK_LIMIT = 64_000_000
KERNEL_LIMIT = 14 << 20

VMEM = pl.BlockSpec(memory_space=pltpu.VMEM)
SMEM = pl.BlockSpec(memory_space=pltpu.SMEM)
HBM = pl.BlockSpec(memory_space=pltpu.HBM)


def lane_index(shape):
    return lax.broadcasted_iota(jnp.int32, shape, len(shape) - 1)


def pack_query_kernel(targets, plan_hbm, query_hbm, *refs):
    outs, (plan_ref, query_ref, sems) = refs[:-3], refs[-3:]
    plan_copy = pltpu.make_async_copy(plan_hbm, plan_ref, sems.at[0])
    query_copy = pltpu.make_async_copy(query_hbm, query_ref, sems.at[1])
    plan_copy.start()
    query_copy.start()
    me = lax.axis_index("dp")
    heads = query_ref.shape[1]
    half = heads // 2
    plan_copy.wait()
    query_copy.wait()
    for k, out in zip(targets, outs):
        r = plan_ref[me ^ k]
        for i in range(TILES):
            out[i * heads:(i + 1) * heads, :] = query_ref[r, :, i * LANES:(i + 1) * LANES]
        rotary = query_ref[r, :, DL:]
        out[TILES * heads:, :] = jnp.concatenate([rotary[:half], rotary[half:]], axis=1)


def unpack_query(packed_ref, heads):
    latent = jnp.concatenate(
        [packed_ref[i * heads:(i + 1) * heads, :] for i in range(TILES)], axis=1
    )
    tail = packed_ref[TILES * heads:, :]
    rotary = jnp.concatenate([tail[:, : LANES // 2], tail[:, LANES // 2:]], axis=0)
    return latent, rotary


def attend(latent, rotary, keys, length):
    width = keys.shape[1]
    scores = jnp.dot(latent, keys[:DL, :], preferred_element_type=jnp.float32)
    scores = scores + jnp.dot(rotary, keys[DL:, :], preferred_element_type=jnp.float32)
    scores = scores * score_scale
    scores = jnp.where(lane_index((1, width)) < length, scores, masked_score)
    largest = jnp.max(scores, axis=1, keepdims=True)
    exponent = jnp.exp(scores - largest)
    totals = jnp.sum(exponent, axis=1, keepdims=True)
    weights = exponent.astype(jnp.bfloat16)
    weighted = lax.dot_general(
        weights, keys[:DL, :], (((1,), (1,)), ((), ())), preferred_element_type=jnp.float32
    )
    return weighted / totals, largest + jnp.log(totals)


def put_lane(block, lane, column):
    return jnp.where(lane_index(block.shape) == lane, column, block)


def split_three(block):
    high = block.astype(jnp.bfloat16).astype(jnp.float32)
    rest = block - high
    middle = rest.astype(jnp.bfloat16).astype(jnp.float32)
    low = rest - middle
    return high + pltpu.roll(middle, PIECE, 1) + pltpu.roll(low, 2 * PIECE, 1)


def join_three(block):
    return block + pltpu.roll(block, LANES - PIECE, 1) + pltpu.roll(block, LANES - 2 * PIECE, 1)


def put_slot(stage, slot, rows, partial):
    heads = partial.shape[0]
    for i in range(TILES):
        stage[i, pl.ds(slot, heads, stride=rows), :] = partial[:, i * LANES:(i + 1) * LANES]


def write_messages(stage, side, rows, outs, part, other=None, taken=0):
    me = lax.axis_index("sub")
    for k, out in enumerate(outs):
        seat = me ^ k
        start = pl.multiple_of(seat * (part * rows), 8)
        for i in range(TILES):
            chunk = stage[i, pl.ds(start, part * rows), :]
            if taken:
                row = lax.broadcasted_iota(jnp.int32, chunk.shape, 0) % rows
                chunk = jnp.where(row < taken, other[i, pl.ds(start, part * rows), :], chunk)
            out[i * part * rows:(i + 1) * part * rows, :] = chunk.astype(jnp.bfloat16)
        side_start = pl.multiple_of(seat * part, 8)
        out[TILES * part * rows:, :] = side[pl.ds(side_start, part), :].astype(jnp.bfloat16)


def own_kernel(rows, plan_ref, own_len_ref, host_len_ref, query_ref, own_ref, host_ref, cache_ref, stage, table_ref, sems):
    me = lax.axis_index("dp")
    requests, heads, _ = query_ref.shape
    groups = host_ref.shape[0]
    copies = []
    for k in range(groups):
        g = me ^ k
        copies.append(pltpu.make_async_copy(host_ref.at[g], cache_ref.at[g], sems.at[k]))
        copies[k].start()
    table = jnp.zeros((heads, LANES), jnp.float32)
    for r in range(requests):
        query = query_ref[r]
        partial, lse = attend(query[:, :DL], query[:, DL:], own_ref.at[r], own_len_ref[r])
        put_slot(stage, r, rows, partial)
        table = put_lane(table, r, lse)
    copies[0].wait()
    query = query_ref[plan_ref[me]]
    partial, lse = attend(query[:, :DL], query[:, DL:], cache_ref.at[me], host_len_ref[me])
    put_slot(stage, requests, rows, partial)
    table = put_lane(table, requests, lse)
    for p in range(groups):
        table = put_lane(table, PLAN_LANE + p, plan_ref[p].astype(jnp.float32))
    table_ref[...] = table
    for copy in copies[1:]:
        copy.wait()


def near_kernel(near, requests, rows, n_sub, host_len_ref, host_ref, own_stage, table_ref, *refs):
    packed, outs, (stage, side) = refs[: near - 1], refs[near - 1: near - 1 + n_sub], refs[near - 1 + n_sub:]
    me = lax.axis_index("dp")
    heads = side.shape[0]
    table = table_ref[...]
    lane = lane_index(table.shape)
    for k in range(1, near):
        g = me ^ k
        latent, rotary = unpack_query(packed[k - 1], heads)
        partial, lse = attend(latent, rotary, host_ref.at[g], host_len_ref[g])
        put_slot(stage, requests + k, rows, partial)
        table = put_lane(table, requests + k, lse)
    pieces = split_three(jnp.where(lane < PIECE, table, 0.0))
    side[...] = jnp.where(lane < PLAN_LANE, pieces, table)
    write_messages(stage, side, rows, outs, heads // n_sub, own_stage, requests + 1)


def far_kernel(near, rows, n_sub, host_len_ref, host_ref, *refs):
    groups = host_ref.shape[0]
    far = groups - near
    packed, outs, (stage, side) = refs[:far], refs[far: far + n_sub], refs[far + n_sub:]
    me = lax.axis_index("dp")
    heads = side.shape[0]
    table = jnp.zeros((heads, LANES), jnp.float32)
    if rows != far:
        stage[...] = jnp.zeros_like(stage)
    for j in range(far):
        g = me ^ (near + j)
        latent, rotary = unpack_query(packed[j], heads)
        partial, lse = attend(latent, rotary, host_ref.at[g], host_len_ref[g])
        put_slot(stage, j, rows, partial)
        table = put_lane(table, j, lse)
    side[...] = split_three(table)
    write_messages(stage, side, rows, outs, heads // n_sub)


def lift_kernel(near, requests, near_rows, far_rows, n_sub, groups, value_ref, *refs):
    near_in, far_in = refs[:n_sub], refs[n_sub: 2 * n_sub]
    out, own_out, own_side, lhs, lifted = refs[2 * n_sub:]
    me = lax.axis_index("dp")
    part = value_ref.shape[0]
    near_block, far_block = max(near_rows, 8), max(far_rows, 8)
    seats = n_sub * part
    for h in range(part):
        offset = 0
        for sources, rows, block in ((near_in, near_rows, near_block), (far_in, far_rows, far_block)):
            start = h * rows // block * block
            for source in sources:
                for i in range(TILES):
                    base = i * part * rows + start
                    lhs[h, offset: offset + block, i * LANES:(i + 1) * LANES] = source[base: base + block, :]
                offset += block
        result = jnp.dot(lhs[h], value_ref[h], preferred_element_type=jnp.float32)
        for s in range(n_sub):
            base = s * near_block
            lifted[pl.ds(s * part + h, near_block, stride=seats), :] = result[base: base + near_block]
            base = n_sub * near_block + s * far_block
            piece = result[base: base + far_block]
            skip = h * far_rows % far_block
            if skip:
                piece = pltpu.roll(piece, far_block - skip, 0)
            lifted[pl.ds(near_block * seats + s * part + h, far_block, stride=seats), :] = piece
    side_near = [ref[TILES * part * near_rows:, :].astype(jnp.float32) for ref in near_in]
    side_far = [ref[TILES * part * far_rows:, :].astype(jnp.float32) for ref in far_in]
    lane = lane_index((part, LANES))
    for k in range(groups):
        g = me ^ k
        row = requests + k if k < near else k - near
        first = (row if k < near else near_block + row) * seats
        out[g, :seats, :] = lifted[first: first + seats, :].astype(jnp.bfloat16)
        tile = jnp.zeros((part, LANES), jnp.float32)
        for s in range(n_sub):
            source = side_near[s] if k < near else side_far[s]
            moved = pltpu.roll(source, (s - row) % LANES, 1) if s != row else source
            tile = jnp.where((lane % PIECE == s) & (lane < 3 * PIECE), moved, tile)
        out[g, seats:, :] = tile.astype(jnp.bfloat16)
    own_out[...] = lifted[: requests * seats, :]
    for s in range(n_sub):
        own_side[s] = side_near[s]


def finish_kernel(requests, n_sub, groups, back_ref, own_ref, side_ref, out_ref):
    part = out_ref.shape[1]
    seats = n_sub * part
    lane = lane_index((part, LANES))
    sides = [side_ref[s] for s in range(n_sub)]
    joined = [join_three(side) for side in sides]
    help_lse, help_plan = [], []
    for p in range(groups):
        help_lse.append(join_three(back_ref[p, seats:, :].astype(jnp.float32)))
        plan = jnp.full((part, LANES), -1.0, jnp.float32)
        for s in range(n_sub):
            plan = put_lane(plan, s, sides[s][:, PLAN_LANE + p: PLAN_LANE + p + 1])
        help_plan.append(plan)
    peaks = []
    owns = []
    for r in range(requests):
        own = jnp.full((part, LANES), masked_score, jnp.float32)
        for s in range(n_sub):
            own = put_lane(own, s, joined[s][:, r: r + 1])
        peak = own
        for p in range(groups):
            peak = jnp.maximum(peak, jnp.where(help_plan[p] == r, help_lse[p], masked_score))
        peaks.append(jnp.max(peak, axis=1, keepdims=True))
        owns.append(own)
    for r in range(requests):
        own_weight = jnp.where(lane < n_sub, jnp.exp(owns[r] - peaks[r]), 0.0)
        total = own_weight
        summed = jnp.zeros((part, LANES), jnp.float32)
        for s in range(n_sub):
            first = (r * n_sub + s) * part
            summed = summed + own_weight[:, s: s + 1] * own_ref[first: first + part, :]
        for p in range(groups):
            chosen = help_plan[p] == r
            weight = jnp.exp(jnp.where(chosen, help_lse[p] - peaks[r], masked_score))
            total = total + weight
            for s in range(n_sub):
                value = back_ref[p, s * part:(s + 1) * part, :].astype(jnp.float32)
                summed = summed + weight[:, s: s + 1] * value
        total = jnp.sum(total, axis=1, keepdims=True)
        out_ref[r] = (summed / total).astype(jnp.bfloat16)


def exchange(array, axis, k):
    size = lax.axis_size(axis)
    return lax.ppermute(array, axis, [(i, i ^ k) for i in range(size)])


def call(kernel, outs, in_specs, scratch=(), limit=None, cost=None):
    def run(*args):
        return pl.pallas_call(
            kernel,
            out_shape=outs,
            in_specs=in_specs,
            out_specs=jax.tree.map(lambda _: VMEM, outs),
            scratch_shapes=list(scratch),
            compiler_params=pltpu.CompilerParams(vmem_limit_bytes=limit),
            cost_estimate=cost,
        )(*args)

    return run


def near_count(groups):
    return min(4, groups)


def local(queries, own_cache, own_len, host_cache, host_len, page_plan, value_up):
    groups, n_sub = lax.axis_size("dp"), lax.axis_size("sub")
    requests, heads, width = queries.shape
    part = heads // n_sub
    slot_tokens = host_cache.shape[3]
    near = near_count(groups)
    far = groups - near
    near_rows = requests + near
    far_rows = far if far in (1, 2, 4) else -(-far // 8) * 8
    plan = page_plan.reshape(groups)
    lengths = host_len.reshape(groups)
    own_lengths = own_len.reshape(requests)
    own_keys = jnp.swapaxes(own_cache, 1, 2)
    host_keys = jnp.swapaxes(host_cache.reshape(groups, slot_tokens, width), 1, 2)

    targets = list(range(1, groups))
    packed = jax.ShapeDtypeStruct((heads * width // LANES, LANES), jnp.bfloat16)
    outgoing = call(
        functools.partial(pack_query_kernel, targets), [packed] * len(targets), [HBM, HBM],
        [pltpu.SMEM(plan.shape, plan.dtype), pltpu.VMEM(queries.shape, queries.dtype), pltpu.SemaphoreType.DMA((2,))],
        limit=PACK_LIMIT,
    )(plan, queries)
    order = list(range(near, groups)) + list(range(1, near))
    received = {k: exchange(outgoing[k - 1], "dp", k) for k in order}

    def message(rows):
        return jax.ShapeDtypeStruct((TILES * part * rows + part, LANES), jnp.bfloat16)

    def stage_shape(rows):
        return (TILES, heads * rows, LANES)

    def stages(rows):
        return [pltpu.VMEM(stage_shape(rows), jnp.float32), pltpu.VMEM((heads, LANES), jnp.float32)]

    def cost(slots):
        return pl.CostEstimate(
            flops=2 * slots * heads * slot_tokens * (width + DL),
            bytes_accessed=2 * slots * slot_tokens * width,
            transcendentals=slots * heads * slot_tokens,
        )

    cache, own_stage, table = call(
        functools.partial(own_kernel, near_rows),
        [
            jax.ShapeDtypeStruct(host_keys.shape, host_keys.dtype),
            jax.ShapeDtypeStruct(stage_shape(near_rows), jnp.float32),
            jax.ShapeDtypeStruct((heads, LANES), jnp.float32),
        ],
        [SMEM] * 3 + [VMEM] * 2 + [HBM],
        [pltpu.SemaphoreType.DMA((groups,))],
        limit=OWN_LIMIT,
        cost=cost(groups),
    )(plan, own_lengths, lengths, queries, own_keys, host_keys)
    near_out = call(
        functools.partial(near_kernel, near, requests, near_rows, n_sub),
        [message(near_rows)] * n_sub,
        [SMEM] + [VMEM] * (3 + near - 1),
        stages(near_rows),
        limit=KERNEL_LIMIT,
        cost=cost(near - 1),
    )(lengths, cache, own_stage, table, *[received[k] for k in range(1, near)])
    far_out = call(
        functools.partial(far_kernel, near, far_rows, n_sub),
        [message(far_rows)] * n_sub,
        [SMEM] + [VMEM] * (1 + far),
        stages(far_rows),
        limit=KERNEL_LIMIT,
        cost=cost(far),
    )(lengths, cache, *[received[k] for k in range(near, groups)])
    sub_order = [k for k in range(2, n_sub)] + [1]
    near_in, far_in = {0: near_out[0]}, {0: far_out[0]}
    for k in sub_order:
        near_in[k] = exchange(near_out[k], "sub", k)
    for k in sub_order:
        far_in[k] = exchange(far_out[k], "sub", k)

    near_block, far_block = max(near_rows, 8), max(far_rows, 8)
    seats = n_sub * part
    back, own, side = call(
        functools.partial(lift_kernel, near, requests, near_rows, far_rows, n_sub, groups),
        [
            jax.ShapeDtypeStruct((groups, seats + part, LANES), jnp.bfloat16),
            jax.ShapeDtypeStruct((requests * seats, LANES), jnp.float32),
            jax.ShapeDtypeStruct((n_sub, part, LANES), jnp.float32),
        ],
        [VMEM] * (1 + 2 * n_sub),
        [
            pltpu.VMEM((part, n_sub * (near_block + far_block), DL), jnp.bfloat16),
            pltpu.VMEM(((near_block + far_block) * seats, LANES), jnp.float32),
        ],
        limit=12 << 20,
    )(value_up, *[near_in[k] for k in range(n_sub)], *[far_in[k] for k in range(n_sub)])
    back = lax.all_to_all(back, "dp", split_axis=0, concat_axis=0, tiled=True)
    return call(
        functools.partial(finish_kernel, requests, n_sub, groups),
        jax.ShapeDtypeStruct((requests, part, LANES), jnp.bfloat16),
        [VMEM] * 3,
        limit=4 << 20,
    )(back, own, side)


def solution(mesh):
    return jax.shard_map(
        local,
        mesh=mesh,
        in_specs=(
            P("dp", None, None),
            P("dp", "sub", None),
            P("dp", "sub"),
            P("dp", "sub", None, None, None),
            P("dp", "sub", None),
            P("dp", "sub", None),
            P("sub", None, None),
        ),
        out_specs=P("dp", "sub", None),
        check_vma=False,
    )
```

profile of v0, /device:TPU:0, one launch (start us, length us, event | category | flops | bytes accessed | tf_op | source)
XLA Modules:
  0.0 59.4 jit_solution(9664315353983601649)
XLA Ops:
  0.0 1.9 %shard_map.74 = (bf16[288,128]{1,0:T(8,128)(2,1)}, bf16[288,128]{1,0:T(8,128)(2,1)}, bf16[288,128]{1,0:T(8,128)(2,1)}, bf16[288,128]{1,0:T(8,128)(2,1)}, bf16[28...) custom-call(s32[8]{0:T(128)} %bitcast.11, bf16[4,64,576]{2,1,0:T(8,128)(2,1)} %query_hbm.1), custom_call_target="tpu_custom_call" | custom-call | tf_op jit(solution)/shard_map/pallas_call | solution.py:271
  1.9 4.1 %collective-permute-start.6 = (bf16[288,128]{1,0:T(8,128)(2,1)}, bf16[288,128]{1,0:T(8,128)(2,1)S(1)}, u32[]{:S(2)}, u32[]{:S(2)}) collective-permute-start(bf16[288,128]{1,0:T(8,128)(2,1)} %get-tuple-element.36), channel_id=1, source_target_pairs={{0,16},{4,20},{8,24},{12,28},{16,0},{20,4},{24,8},{28,12},{1,17},{... | collective-permute-start | bytes 221192 | tf_op jit(solution)/shard_map/ppermute | solution.py:266
  6.0 1.3 %collective-permute-start.7 = (bf16[288,128]{1,0:T(8,128)(2,1)}, bf16[288,128]{1,0:T(8,128)(2,1)S(1)}, u32[]{:S(2)}, u32[]{:S(2)}) collective-permute-start(bf16[288,128]{1,0:T(8,128)(2,1)} %get-tuple-element.37), channel_id=1, source_target_pairs={{0,20},{4,16},{8,28},{12,24},{16,4},{20,0},{24,12},{28,8},{1,21},{... | collective-permute-start | bytes 221192 | tf_op jit(solution)/shard_map/ppermute | solution.py:266
  7.3 0.2 collective-permute-start
  7.6 1.8 %collective-permute-start.1 = (bf16[288,128]{1,0:T(8,128)(2,1)}, bf16[288,128]{1,0:T(8,128)(2,1)S(1)}, u32[]{:S(2)}, u32[]{:S(2)}) collective-permute-start(bf16[288,128]{1,0:T(8,128)(2,1)} %get-tuple-element.30), channel_id=1, source_target_pairs={{0,8},{4,12},{8,0},{12,4},{16,24},{20,28},{24,16},{28,20},{1,9},{5... | collective-permute-start | bytes 221192 | tf_op jit(solution)/shard_map/ppermute | solution.py:266
  9.4 1.4 %collective-permute-start.2 = (bf16[288,128]{1,0:T(8,128)(2,1)}, bf16[288,128]{1,0:T(8,128)(2,1)S(1)}, u32[]{:S(2)}, u32[]{:S(2)}) collective-permute-start(bf16[288,128]{1,0:T(8,128)(2,1)} %get-tuple-element.31), channel_id=1, source_target_pairs={{0,12},{4,8},{8,4},{12,0},{16,28},{20,24},{24,20},{28,16},{1,13},{... | collective-permute-start | bytes 221192 | tf_op jit(solution)/shard_map/ppermute | solution.py:266
  10.8 0.0 collective-permute-done.6.refs_0_
  10.8 4.7 %collective-permute-start.8 = (bf16[288,128]{1,0:T(8,128)(2,1)}, bf16[288,128]{1,0:T(8,128)(2,1)S(1)}, u32[]{:S(2)}, u32[]{:S(2)}) collective-permute-start(bf16[288,128]{1,0:T(8,128)(2,1)} %get-tuple-element.38), channel_id=1, source_target_pairs={{0,24},{4,28},{8,16},{12,20},{16,8},{20,12},{24,0},{28,4},{1,25},{... | collective-permute-start | bytes 221192 | tf_op jit(solution)/shard_map/ppermute | solution.py:266
  15.5 0.0 collective-permute-done.7.refs_1_
  15.5 2.4 %collective-permute-start.9 = (bf16[288,128]{1,0:T(8,128)(2,1)}, bf16[288,128]{1,0:T(8,128)(2,1)S(1)}, u32[]{:S(2)}, u32[]{:S(2)}) collective-permute-start(bf16[288,128]{1,0:T(8,128)(2,1)} %get-tuple-element.39), channel_id=1, source_target_pairs={{0,28},{4,24},{8,20},{12,16},{16,12},{20,8},{24,4},{28,0},{1,29},{... | collective-permute-start | bytes 221192 | tf_op jit(solution)/shard_map/ppermute | solution.py:266
  18.0 0.0 copy-start.1
  18.0 1.0 %copy-done.1 = bf16[4,64,576]{2,1,0:T(8,128)(2,1)S(1)} copy-done((bf16[4,64,576]{2,1,0:T(8,128)(2,1)S(1)}, bf16[4,64,576]{2,1,0:T(8,128)(2,1)}, u32[]{:S(2)}) %copy-start.1) | copy-done | bytes 294936
  18.9 0.0 copy-start.2
  18.9 1.3 %copy-done.2 = bf16[4,256,576]{1,2,0:T(8,128)(2,1)S(1)} copy-done((bf16[4,256,576]{1,2,0:T(8,128)(2,1)S(1)}, bf16[4,256,576]{1,2,0:T(8,128)(2,1)}, u32[]{:S(2)}) %copy-start.2) | copy-done | bytes 1179672
  20.2 0.0 copy-start.3
  20.2 0.7 %copy-done.3 = s32[1,1,8]{2,1,0:T(1,128)S(1)} copy-done((s32[1,1,8]{2,1,0:T(1,128)S(1)}, s32[1,1,8]{2,1,0:T(1,128)}, u32[]{:S(2)}) %copy-start.3) | copy-done | bytes 56
  20.9 0.0 copy-start.4
  20.9 0.7 %copy-done.4 = s32[1,1,8]{2,1,0:T(1,128)S(1)} copy-done((s32[1,1,8]{2,1,0:T(1,128)S(1)}, s32[1,1,8]{2,1,0:T(1,128)}, u32[]{:S(2)}) %copy-start.4) | copy-done | bytes 56
  21.5 0.0 copy-start.5
  21.5 0.7 %copy-done.5 = s32[4,1]{0,1:T(1,128)S(1)} copy-done((s32[4,1]{0,1:T(1,128)S(1)}, s32[4,1]{0,1:T(1,128)}, u32[]{:S(2)}) %copy-start.5) | copy-done | bytes 40
  22.2 5.4 %shard_map.73 = (bf16[8,576,1024]{2,1,0:T(8,128)(2,1)S(1)}, f32[4,512,128]{2,1,0:T(8,128)S(1)}, f32[64,128]{1,0:T(8,128)S(1)}) custom-call(s32[8]{0:T(128)S(1)} %bitcast.12, s32[4]{0:T(128)S(1)} %bitcast.13, s32[8]{0:T(128)S(1)} %bitcast.8, bf16[4,64,576]{2,1,0:T(8,128)(2,1)S(1)} %copy-done.1, bf16[4,576,256]{2,1,0:T(8,128)(2,1)S(1)} %bitcast.7, ...), custom_call_target="tpu_custom_call" | custom-call | flops 1140850688 | bytes 9437184 | tf_op jit(solution)/shard_map/pallas_call | solution.py:271
  27.6 0.0 collective-permute-done.8.refs_2_
  27.6 0.0 collective-permute-done.9.refs_3_
  27.6 0.0 copy-start
  27.6 3.5 %shard_map.76 = (bf16[272,128]{1,0:T(8,128)(2,1)S(1)}, bf16[272,128]{1,0:T(8,128)(2,1)S(1)}, bf16[272,128]{1,0:T(8,128)(2,1)S(1)}, bf16[272,128]{1,0:T(8,128)(2,1)S(1)}) custom-call(s32[8]{0:T(128)S(1)} %bitcast.9, bf16[8,576,1024]{2,1,0:T(8,128)(2,1)S(1)} %get-tuple-element.26.host_ref, bf16[288,128]{1,0:T(8,128)(2,1)S(1)} %collective-permute-done.6.refs_0_, ...), custom_call_target="tpu_custom_call" | custom-call | flops 570425344 | bytes 4718592 | tf_op jit(solution)/shard_map/pallas_call | solution.py:271
  31.1 0.1 collective-permute-start.10
  31.2 0.0 collective-permute-done.refs_0_
  31.2 0.0 collective-permute-done.1.refs_1_
  31.2 0.0 collective-permute-done.2.refs_2_
  31.2 2.9 %shard_map.75 = (bf16[528,128]{1,0:T(8,128)(2,1)S(1)}, bf16[528,128]{1,0:T(8,128)(2,1)S(1)}, bf16[528,128]{1,0:T(8,128)(2,1)S(1)}, bf16[528,128]{1,0:T(8,128)(2,1)S(1)}) custom-call(s32[8]{0:T(128)S(1)} %bitcast.10, bf16[8,576,1024]{2,1,0:T(8,128)(2,1)S(1)} %get-tuple-element.26.host_ref, f32[4,512,128]{2,1,0:T(8,128)S(1)} %get-tuple-element.27.own_stage, ...), custom_call_target="tpu_custom_call" | custom-call | flops 427819008 | bytes 3538944 | tf_op jit(solution)/shard_map/pallas_call | solution.py:271
  34.1 0.5 collective-permute-start.3
  34.7 1.5 %collective-permute-start.4 = (bf16[528,128]{1,0:T(8,128)(2,1)S(1)}, bf16[528,128]{1,0:T(8,128)(2,1)S(1)}, u32[]{:S(2)}, u32[]{:S(2)}) collective-permute-start(bf16[528,128]{1,0:T(8,128)(2,1)S(1)} %get-tuple-element.34), channel_id=1, source_target_pairs={{0,2},{1,3},{2,0},{3,1},{4,6},{5,7},{6,4},{7,5},{8,10},{9,11},{10,... | collective-permute-start | bytes 405512 | tf_op jit(solution)/shard_map/ppermute | solution.py:266
  36.1 0.0 collective-permute-start.5
  36.1 1.4 %collective-permute-start.11 = (bf16[272,128]{1,0:T(8,128)(2,1)S(1)}, bf16[272,128]{1,0:T(8,128)(2,1)S(1)}, u32[]{:S(2)}, u32[]{:S(2)}) collective-permute-start(bf16[272,128]{1,0:T(8,128)(2,1)S(1)} %get-tuple-element.42), channel_id=1, source_target_pairs={{0,2},{1,3},{2,0},{3,1},{4,6},{5,7},{6,4},{7,5},{8,10},{9,11},{10,... | collective-permute-start | bytes 208904 | tf_op jit(solution)/shard_map/ppermute | solution.py:266
  37.6 0.0 collective-permute-done.10.refs_5_
  37.6 0.6 collective-permute-start.12
  38.2 7.2 %collective-permute-done.11.refs_6_ = bf16[272,128]{1,0:T(8,128)(2,1)S(1)} collective-permute-done((bf16[272,128]{1,0:T(8,128)(2,1)S(1)}, bf16[272,128]{1,0:T(8,128)(2,1)S(1)}, u32[]{:S(2)}, u32[]{:S(2)}) %collective-permute-start.11) | collective-permute-done | bytes 69664 | tf_op jit(solution)/shard_map/ppermute | solution.py:266
  45.4 0.0 collective-permute-done.12.refs_7_
  45.4 0.0 collective-permute-done.3.refs_1_
  45.4 0.0 collective-permute-done.4.refs_2_
  45.4 0.0 collective-permute-done.5.refs_3_
  45.4 0.0 copy-done
  45.4 0.7 %shard_map.77 = (bf16[8,80,128]{2,1,0:T(8,128)(2,1)S(1)}, f32[256,128]{1,0:T(8,128)S(1)}, f32[4,16,128]{2,1,0:T(8,128)S(1)}) custom-call(bf16[16,512,128]{2,1,0:T(8,128)(2,1)S(1)} %copy-done, bf16[528,128]{1,0:T(8,128)(2,1)S(1)} %get-tuple-element.32.refs_0_, bf16[528,128]{1,0:T(8,128)(2,1)S(1)} %collective-permute-done.3.refs_1_, ...), custom_call_target="tpu_custom_call" | custom-call | tf_op jit(solution)/shard_map/pallas_call | solution.py:271
  46.1 11.6 %all_to_all.5.back_ref = bf16[8,80,128]{2,1,0:T(8,128)(2,1)S(1)} all-to-all(bf16[8,80,128]{2,1,0:T(8,128)(2,1)S(1)} %get-tuple-element.44), channel_id=1, replica_groups=mesh['dp'=8,'sub'=4] {'dp'}, dimensions={0} | all-to-all | bytes 327680 | tf_op jit(solution)/shard_map/all_to_all | solution.py:380
  57.7 1.7 %shard_map.78 = bf16[4,16,128]{2,1,0:T(8,128)(2,1)} custom-call(bf16[8,80,128]{2,1,0:T(8,128)(2,1)S(1)} %all_to_all.5.back_ref, f32[256,128]{1,0:T(8,128)S(1)} %get-tuple-element.45.own_ref, f32[4,16,128]{2,1,0:T(8,128)S(1)} %get-tuple-element.46.side_ref), custom_call_target="tpu_custom_call" | custom-call | tf_op jit(solution)/shard_map/pallas_call | solution.py:271
Async XLA Ops:
  1.9 8.9 %collective-permute-start.6 = (bf16[288,128]{1,0:T(8,128)(2,1)}, bf16[288,128]{1,0:T(8,128)(2,1)S(1)}, u32[]{:S(2)}, u32[]{:S(2)}) collective-permute-start(bf16[288,128]{1,0:T(8,128)(2,1)} %get-tuple-element.36), channel_id=1, source_target_pairs={{0,16},{4,20},{8,24},{12,28},{16,0},{20,4},{24,8},{28,12},{1,17},{... | collective-permute-start | bytes 221192 | tf_op jit(solution)/shard_map/ppermute | solution.py:266
  6.0 9.5 %collective-permute-start.7 = (bf16[288,128]{1,0:T(8,128)(2,1)}, bf16[288,128]{1,0:T(8,128)(2,1)S(1)}, u32[]{:S(2)}, u32[]{:S(2)}) collective-permute-start(bf16[288,128]{1,0:T(8,128)(2,1)} %get-tuple-element.37), channel_id=1, source_target_pairs={{0,20},{4,16},{8,28},{12,24},{16,4},{20,0},{24,12},{28,8},{1,21},{... | collective-permute-start | bytes 221192 | tf_op jit(solution)/shard_map/ppermute | solution.py:266
  7.3 23.8 %collective-permute-start = (bf16[288,128]{1,0:T(8,128)(2,1)}, bf16[288,128]{1,0:T(8,128)(2,1)S(1)}, u32[]{:S(2)}, u32[]{:S(2)}) collective-permute-start(bf16[288,128]{1,0:T(8,128)(2,1)} %get-tuple-element.29), channel_id=1, source_target_pairs={{0,4},{4,0},{8,12},{12,8},{16,20},{20,16},{24,28},{28,24},{1,5},{5... | collective-permute-start | bytes 221192 | tf_op jit(solution)/shard_map/ppermute | solution.py:266
  7.6 23.6 %collective-permute-start.1 = (bf16[288,128]{1,0:T(8,128)(2,1)}, bf16[288,128]{1,0:T(8,128)(2,1)S(1)}, u32[]{:S(2)}, u32[]{:S(2)}) collective-permute-start(bf16[288,128]{1,0:T(8,128)(2,1)} %get-tuple-element.30), channel_id=1, source_target_pairs={{0,8},{4,12},{8,0},{12,4},{16,24},{20,28},{24,16},{28,20},{1,9},{5... | collective-permute-start | bytes 221192 | tf_op jit(solution)/shard_map/ppermute | solution.py:266
  9.4 21.8 %collective-permute-start.2 = (bf16[288,128]{1,0:T(8,128)(2,1)}, bf16[288,128]{1,0:T(8,128)(2,1)S(1)}, u32[]{:S(2)}, u32[]{:S(2)}) collective-permute-start(bf16[288,128]{1,0:T(8,128)(2,1)} %get-tuple-element.31), channel_id=1, source_target_pairs={{0,12},{4,8},{8,4},{12,0},{16,28},{20,24},{24,20},{28,16},{1,13},{... | collective-permute-start | bytes 221192 | tf_op jit(solution)/shard_map/ppermute | solution.py:266
  10.8 16.8 %collective-permute-start.8 = (bf16[288,128]{1,0:T(8,128)(2,1)}, bf16[288,128]{1,0:T(8,128)(2,1)S(1)}, u32[]{:S(2)}, u32[]{:S(2)}) collective-permute-start(bf16[288,128]{1,0:T(8,128)(2,1)} %get-tuple-element.38), channel_id=1, source_target_pairs={{0,24},{4,28},{8,16},{12,20},{16,8},{20,12},{24,0},{28,4},{1,25},{... | collective-permute-start | bytes 221192 | tf_op jit(solution)/shard_map/ppermute | solution.py:266
  15.5 12.0 %collective-permute-start.9 = (bf16[288,128]{1,0:T(8,128)(2,1)}, bf16[288,128]{1,0:T(8,128)(2,1)S(1)}, u32[]{:S(2)}, u32[]{:S(2)}) collective-permute-start(bf16[288,128]{1,0:T(8,128)(2,1)} %get-tuple-element.39), channel_id=1, source_target_pairs={{0,28},{4,24},{8,20},{12,16},{16,12},{20,8},{24,4},{28,0},{1,29},{... | collective-permute-start | bytes 221192 | tf_op jit(solution)/shard_map/ppermute | solution.py:266
  18.0 1.0 %copy-start.1 = (bf16[4,64,576]{2,1,0:T(8,128)(2,1)S(1)}, bf16[4,64,576]{2,1,0:T(8,128)(2,1)}, u32[]{:S(2)}) copy-start(bf16[4,64,576]{2,1,0:T(8,128)(2,1)} %query_hbm.1) | copy-start | bytes 884740
  18.9 1.3 %copy-start.2 = (bf16[4,256,576]{1,2,0:T(8,128)(2,1)S(1)}, bf16[4,256,576]{1,2,0:T(8,128)(2,1)}, u32[]{:S(2)}) copy-start(bf16[4,256,576]{1,2,0:T(8,128)(2,1)} %param.8) | copy-start | bytes 3538948
  20.2 0.7 %copy-start.3 = (s32[1,1,8]{2,1,0:T(1,128)S(1)}, s32[1,1,8]{2,1,0:T(1,128)}, u32[]{:S(2)}) copy-start(s32[1,1,8]{2,1,0:T(1,128)} %param.11) | copy-start | bytes 100
  20.9 0.7 %copy-start.4 = (s32[1,1,8]{2,1,0:T(1,128)S(1)}, s32[1,1,8]{2,1,0:T(1,128)}, u32[]{:S(2)}) copy-start(s32[1,1,8]{2,1,0:T(1,128)} %param.12) | copy-start | bytes 100
  21.5 0.7 %copy-start.5 = (s32[4,1]{0,1:T(1,128)S(1)}, s32[4,1]{0,1:T(1,128)}, u32[]{:S(2)}) copy-start(s32[4,1]{0,1:T(1,128)} %param.9) | copy-start | bytes 52
  27.6 17.8 %copy-start = (bf16[16,512,128]{2,1,0:T(8,128)(2,1)S(1)}, bf16[16,512,128]{2,1,0:T(8,128)(2,1)}, u32[]{:S(2)}) copy-start(bf16[16,512,128]{2,1,0:T(8,128)(2,1)} %value_ref.1) | copy-start | bytes 6291460
  31.1 6.5 %collective-permute-start.10 = (bf16[272,128]{1,0:T(8,128)(2,1)S(1)}, bf16[272,128]{1,0:T(8,128)(2,1)S(1)}, u32[]{:S(2)}, u32[]{:S(2)}) collective-permute-start(bf16[272,128]{1,0:T(8,128)(2,1)S(1)} %get-tuple-element.41), channel_id=1, source_target_pairs={{0,1},{1,0},{2,3},{3,2},{4,5},{5,4},{6,7},{7,6},{8,9},{9,8},{10,11... | collective-permute-start | bytes 208904 | tf_op jit(solution)/shard_map/ppermute | solution.py:266
  34.1 11.3 %collective-permute-start.3 = (bf16[528,128]{1,0:T(8,128)(2,1)S(1)}, bf16[528,128]{1,0:T(8,128)(2,1)S(1)}, u32[]{:S(2)}, u32[]{:S(2)}) collective-permute-start(bf16[528,128]{1,0:T(8,128)(2,1)S(1)} %get-tuple-element.33), channel_id=1, source_target_pairs={{0,1},{1,0},{2,3},{3,2},{4,5},{5,4},{6,7},{7,6},{8,9},{9,8},{10,11... | collective-permute-start | bytes 405512 | tf_op jit(solution)/shard_map/ppermute | solution.py:266
  34.7 10.7 %collective-permute-start.4 = (bf16[528,128]{1,0:T(8,128)(2,1)S(1)}, bf16[528,128]{1,0:T(8,128)(2,1)S(1)}, u32[]{:S(2)}, u32[]{:S(2)}) collective-permute-start(bf16[528,128]{1,0:T(8,128)(2,1)S(1)} %get-tuple-element.34), channel_id=1, source_target_pairs={{0,2},{1,3},{2,0},{3,1},{4,6},{5,7},{6,4},{7,5},{8,10},{9,11},{10,... | collective-permute-start | bytes 405512 | tf_op jit(solution)/shard_map/ppermute | solution.py:266
  36.1 9.2 %collective-permute-start.5 = (bf16[528,128]{1,0:T(8,128)(2,1)S(1)}, bf16[528,128]{1,0:T(8,128)(2,1)S(1)}, u32[]{:S(2)}, u32[]{:S(2)}) collective-permute-start(bf16[528,128]{1,0:T(8,128)(2,1)S(1)} %get-tuple-element.35), channel_id=1, source_target_pairs={{0,3},{1,2},{2,1},{3,0},{4,7},{5,6},{6,5},{7,4},{8,11},{9,10},{10,... | collective-permute-start | bytes 405512 | tf_op jit(solution)/shard_map/ppermute | solution.py:266
  36.1 9.2 %collective-permute-start.11 = (bf16[272,128]{1,0:T(8,128)(2,1)S(1)}, bf16[272,128]{1,0:T(8,128)(2,1)S(1)}, u32[]{:S(2)}, u32[]{:S(2)}) collective-permute-start(bf16[272,128]{1,0:T(8,128)(2,1)S(1)} %get-tuple-element.42), channel_id=1, source_target_pairs={{0,2},{1,3},{2,0},{3,1},{4,6},{5,7},{6,4},{7,5},{8,10},{9,11},{10,... | collective-permute-start | bytes 208904 | tf_op jit(solution)/shard_map/ppermute | solution.py:266
  37.6 7.8 %collective-permute-start.12 = (bf16[272,128]{1,0:T(8,128)(2,1)S(1)}, bf16[272,128]{1,0:T(8,128)(2,1)S(1)}, u32[]{:S(2)}, u32[]{:S(2)}) collective-permute-start(bf16[272,128]{1,0:T(8,128)(2,1)S(1)} %get-tuple-element.43), channel_id=1, source_target_pairs={{0,3},{1,2},{2,1},{3,0},{4,7},{5,6},{6,5},{7,4},{8,11},{9,10},{10,... | collective-permute-start | bytes 208904 | tf_op jit(solution)/shard_map/ppermute | solution.py:266
where the time goes:
time: 59.7 us; the launch traced here: 59.4 us
  starting transfers between devices  20.2 us (34%)
  Pallas kernels  16.1 us (27%)
  blocking collectives  11.6 us (19%)
  waiting for transfers between devices  7.24 us (12%)
  local copies, waits for them, and re-layouts  4.21 us (7%)
    ppermute x13, starting transfers between devices, exchange(): return lax.ppermute(array, axis, [(i, i ^ k) for i in range(size)])  20.2 us
    pallas_call x6, Pallas kernels, run(): pl.pallas_call(kernel, out_shape=outs, in_specs=in_specs, out_specs=jax.t...  16.1 us
    all_to_all x1, blocking collectives, local(): back = lax.all_to_all(back, 'dp', split_axis=0, concat_axis=0, tiled=True)  11.6 us
    ppermute x13, waiting for transfers between devices, exchange(): return lax.ppermute(array, axis, [(i, i ^ k) for i in range(size)])  7.24 us
    unnamed x12, local copies, waits for them, and re-layouts  4.21 us
  transfers between devices with their start and end apart: 13, of which 1 were waited for; matrix products, arithmetic and copies ran while one was open for 0% of the time, Pallas kernels for 20%

commit v1 on v0

--- a/solution.py
+++ b/solution.py
@@ -17,8 +17,8 @@
 masked_score = -1e30
 
 
-OWN_LIMIT = 42 << 20
-PACK_LIMIT = 64_000_000
+OWN_LIMIT = 24 << 20
+PACK_LIMIT = 2 << 20
 KERNEL_LIMIT = 14 << 20
 
 VMEM = pl.BlockSpec(memory_space=pltpu.VMEM)
@@ -111,15 +111,25 @@
         out[TILES * part * rows:, :] = side[pl.ds(side_start, part), :].astype(jnp.bfloat16)
 
 
-def own_kernel(rows, plan_ref, own_len_ref, host_len_ref, query_ref, own_ref, host_ref, cache_ref, stage, table_ref, sems):
+def own_kernel(rows, plan_hbm, own_len_hbm, host_len_hbm, query_hbm, own_hbm, host_ref, cache_ref, stage, table_ref,
+               plan_ref, own_len_ref, host_len_ref, query_ref, own_ref, first_sems, sems):
     me = lax.axis_index("dp")
-    requests, heads, _ = query_ref.shape
     groups = host_ref.shape[0]
+    firsts = []
+    for i, (source, target) in enumerate((
+        (query_hbm, query_ref), (own_hbm, own_ref), (plan_hbm, plan_ref),
+        (own_len_hbm, own_len_ref), (host_len_hbm, host_len_ref),
+    )):
+        firsts.append(pltpu.make_async_copy(source, target, first_sems.at[i]))
+        firsts[i].start()
     copies = []
     for k in range(groups):
         g = me ^ k
         copies.append(pltpu.make_async_copy(host_ref.at[g], cache_ref.at[g], sems.at[k]))
         copies[k].start()
+    requests, heads, _ = query_ref.shape
+    for copy in firsts:
+        copy.wait()
     table = jnp.zeros((heads, LANES), jnp.float32)
     for r in range(requests):
         query = query_ref[r]
@@ -281,6 +291,10 @@
     return run
 
 
+def in_hbm(array):
+    return pltpu.with_memory_space_constraint(array, pltpu.HBM)
+
+
 def near_count(groups):
     return min(4, groups)
 
@@ -306,7 +320,7 @@
         functools.partial(pack_query_kernel, targets), [packed] * len(targets), [HBM, HBM],
         [pltpu.SMEM(plan.shape, plan.dtype), pltpu.VMEM(queries.shape, queries.dtype), pltpu.SemaphoreType.DMA((2,))],
         limit=PACK_LIMIT,
-    )(plan, queries)
+    )(in_hbm(plan), in_hbm(queries))
     order = list(range(near, groups)) + list(range(1, near))
     received = {k: exchange(outgoing[k - 1], "dp", k) for k in order}
 
@@ -333,11 +347,19 @@
             jax.ShapeDtypeStruct(stage_shape(near_rows), jnp.float32),
             jax.ShapeDtypeStruct((heads, LANES), jnp.float32),
         ],
-        [SMEM] * 3 + [VMEM] * 2 + [HBM],
-        [pltpu.SemaphoreType.DMA((groups,))],
+        [HBM] * 6,
+        [
+            pltpu.SMEM(plan.shape, plan.dtype),
+            pltpu.SMEM(own_lengths.shape, own_lengths.dtype),
+            pltpu.SMEM(lengths.shape, lengths.dtype),
+            pltpu.VMEM(queries.shape, queries.dtype),
+            pltpu.VMEM(own_keys.shape, own_keys.dtype),
+            pltpu.SemaphoreType.DMA((5,)),
+            pltpu.SemaphoreType.DMA((groups,)),
+        ],
         limit=OWN_LIMIT,
         cost=cost(groups),
-    )(plan, own_lengths, lengths, queries, own_keys, host_keys)
+    )(*[in_hbm(x) for x in (plan, own_lengths, lengths, queries, own_keys, host_keys)])
     near_out = call(
         functools.partial(near_kernel, near, requests, near_rows, n_sub),
         [message(near_rows)] * n_sub,

time: 59.7 us -> 53.8 us (0.901)
  local copies, waits for them, and re-layouts: 4.21 us -> 0.01 us
  Pallas kernels: 16.1 us -> 14.2 us
    unnamed x12 -> x4, local copies, waits for them, and re-layouts: 4.21 us -> 0.01 us
    pallas_call x6, Pallas kernels: 16.1 us -> 14.2 us  [run(): pl.pallas_call(kernel, out_shape=outs, in_specs=in_specs, out_specs=jax.t...]
  transfers between devices with their start and end apart: 13 -> 13, of which waited for: 1 -> 2; matrix products, arithmetic and copies ran while one was open for 0% -> 0% of each run, Pallas kernels for 20% -> 20%
where the time goes in v1:
time: 53.8 us; the launch traced here: 53.6 us
  starting transfers between devices  20 us (37%)
  Pallas kernels  14.2 us (26%)
  blocking collectives  11.7 us (22%)
  waiting for transfers between devices  7.58 us (14%)
    ppermute x13, starting transfers between devices, exchange(): return lax.ppermute(array, axis, [(i, i ^ k) for i in range(size)])  20 us
    pallas_call x6, Pallas kernels, run(): pl.pallas_call(kernel, out_shape=outs, in_specs=in_specs, out_specs=jax.t...  14.2 us
    all_to_all x1, blocking collectives, local(): back = lax.all_to_all(back, 'dp', split_axis=0, concat_axis=0, tiled=True)  11.7 us
    ppermute x13, waiting for transfers between devices, exchange(): return lax.ppermute(array, axis, [(i, i ^ k) for i in range(size)])  7.58 us
  transfers between devices with their start and end apart: 13, of which 2 were waited for; matrix products, arithmetic and copies ran while one was open for 0% of the time, Pallas kernels for 20%

profile of v1, /device:TPU:0, one launch (start us, length us, event | category | flops | bytes accessed | tf_op | source)
XLA Modules:
  0.0 53.6 jit_solution(10105841481404476570)
XLA Ops:
  0.0 0.0 copy-start.1
  0.0 1.2 %shard_map.74 = (bf16[288,128]{1,0:T(8,128)(2,1)S(1)}, bf16[288,128]{1,0:T(8,128)(2,1)S(1)}, bf16[288,128]{1,0:T(8,128)(2,1)S(1)}, bf16[288,128]{1,0:T(8,128)(2,...) custom-call(s32[8]{0:T(128)} %bitcast.12, ...), custom_call_target="tpu_custom_call" | custom-call | tf_op jit(solution)/shard_map/pallas_call | solution.py:281
  1.2 4.1 %collective-permute-start.6 = (bf16[288,128]{1,0:T(8,128)(2,1)S(1)}, bf16[288,128]{1,0:T(8,128)(2,1)S(1)}, u32[]{:S(2)}, u32[]{:S(2)}) collective-permute-start(bf16[288,128]{1,0:T(8,128)(2,1)S(1)} %get-tuple-element.36), channel_id=1, source_target_pairs={{0,16},{4,20},{8,24},{12,28},{16,0},{20,4},{24,8},{28,12},{1,17},{... | collective-permute-start | bytes 221192 | tf_op jit(solution)/shard_map/ppermute | solution.py:276
  5.3 1.3 %collective-permute-start.7 = (bf16[288,128]{1,0:T(8,128)(2,1)S(1)}, bf16[288,128]{1,0:T(8,128)(2,1)S(1)}, u32[]{:S(2)}, u32[]{:S(2)}) collective-permute-start(bf16[288,128]{1,0:T(8,128)(2,1)S(1)} %get-tuple-element.37), channel_id=1, source_target_pairs={{0,20},{4,16},{8,28},{12,24},{16,4},{20,0},{24,12},{28,8},{1,21},{... | collective-permute-start | bytes 221192 | tf_op jit(solution)/shard_map/ppermute | solution.py:276
  6.6 0.2 collective-permute-start
  6.8 1.8 %collective-permute-start.1 = (bf16[288,128]{1,0:T(8,128)(2,1)S(1)}, bf16[288,128]{1,0:T(8,128)(2,1)S(1)}, u32[]{:S(2)}, u32[]{:S(2)}) collective-permute-start(bf16[288,128]{1,0:T(8,128)(2,1)S(1)} %get-tuple-element.30), channel_id=1, source_target_pairs={{0,8},{4,12},{8,0},{12,4},{16,24},{20,28},{24,16},{28,20},{1,9},{5... | collective-permute-start | bytes 221192 | tf_op jit(solution)/shard_map/ppermute | solution.py:276
  8.7 1.4 %collective-permute-start.2 = (bf16[288,128]{1,0:T(8,128)(2,1)S(1)}, bf16[288,128]{1,0:T(8,128)(2,1)S(1)}, u32[]{:S(2)}, u32[]{:S(2)}) collective-permute-start(bf16[288,128]{1,0:T(8,128)(2,1)S(1)} %get-tuple-element.31), channel_id=1, source_target_pairs={{0,12},{4,8},{8,4},{12,0},{16,28},{20,24},{24,20},{28,16},{1,13},{... | collective-permute-start | bytes 221192 | tf_op jit(solution)/shard_map/ppermute | solution.py:276
  10.1 0.0 collective-permute-done.6.refs_0_
  10.1 4.5 %collective-permute-start.8 = (bf16[288,128]{1,0:T(8,128)(2,1)S(1)}, bf16[288,128]{1,0:T(8,128)(2,1)S(1)}, u32[]{:S(2)}, u32[]{:S(2)}) collective-permute-start(bf16[288,128]{1,0:T(8,128)(2,1)S(1)} %get-tuple-element.38), channel_id=1, source_target_pairs={{0,24},{4,28},{8,16},{12,20},{16,8},{20,12},{24,0},{28,4},{1,25},{... | collective-permute-start | bytes 221192 | tf_op jit(solution)/shard_map/ppermute | solution.py:276
  14.6 0.0 collective-permute-done.7.refs_1_
  14.6 2.4 %collective-permute-start.9 = (bf16[288,128]{1,0:T(8,128)(2,1)S(1)}, bf16[288,128]{1,0:T(8,128)(2,1)S(1)}, u32[]{:S(2)}, u32[]{:S(2)}) collective-permute-start(bf16[288,128]{1,0:T(8,128)(2,1)S(1)} %get-tuple-element.39), channel_id=1, source_target_pairs={{0,28},{4,24},{8,20},{12,16},{16,12},{20,8},{24,4},{28,0},{1,29},{... | collective-permute-start | bytes 221192 | tf_op jit(solution)/shard_map/ppermute | solution.py:276
  17.0 4.3 %shard_map.73 = (bf16[8,576,1024]{2,1,0:T(8,128)(2,1)S(1)}, f32[4,512,128]{2,1,0:T(8,128)S(1)}, f32[64,128]{1,0:T(8,128)S(1)}) custom-call(s32[8]{0:T(128)} %bitcast.13, s32[4]{0:T(128)} %bitcast.14, s32[8]{0:T(128)} %bitcast.7, bf16[4,64,576]{2,1,0:T(8,128)(2,1)} %query_hbm.3, bf16[4,576,256]{2,1,0:T(8,128)(2,1)} %bitcast.11, bf16[8,576,1024]{2,1,0:T(8,128)(2,1)} %bitcast.10), custom_call_target="tpu_custom_call" | custom-call | flops 1140850688 | bytes 9437184 | tf_op jit(solution)/shard_map/pallas_call | solution.py:281
  21.3 0.0 collective-permute-done.8.refs_2_
  21.3 0.3 collective-permute-done.9.refs_3_
  21.7 0.0 copy-done.1
  21.7 0.0 copy-start
  21.7 3.5 %shard_map.76 = (bf16[272,128]{1,0:T(8,128)(2,1)S(1)}, bf16[272,128]{1,0:T(8,128)(2,1)S(1)}, bf16[272,128]{1,0:T(8,128)(2,1)S(1)}, bf16[272,128]{1,0:T(8,128)(2,1)S(1)}) custom-call(s32[8]{0:T(128)S(1)} %bitcast.8, bf16[8,576,1024]{2,1,0:T(8,128)(2,1)S(1)} %get-tuple-element.26.host_ref, bf16[288,128]{1,0:T(8,128)(2,1)S(1)} %collective-permute-done.6.refs_0_, ...), custom_call_target="tpu_custom_call" | custom-call | flops 570425344 | bytes 4718592 | tf_op jit(solution)/shard_map/pallas_call | solution.py:281
  25.1 0.1 collective-permute-start.10
  25.2 0.0 collective-permute-done.refs_0_
  25.2 0.0 collective-permute-done.1.refs_1_
  25.2 0.0 collective-permute-done.2.refs_2_
  25.2 2.9 %shard_map.75 = (bf16[528,128]{1,0:T(8,128)(2,1)S(1)}, bf16[528,128]{1,0:T(8,128)(2,1)S(1)}, bf16[528,128]{1,0:T(8,128)(2,1)S(1)}, bf16[528,128]{1,0:T(8,128)(2,1)S(1)}) custom-call(s32[8]{0:T(128)S(1)} %bitcast.9, bf16[8,576,1024]{2,1,0:T(8,128)(2,1)S(1)} %get-tuple-element.26.host_ref, f32[4,512,128]{2,1,0:T(8,128)S(1)} %get-tuple-element.27.own_stage, ...), custom_call_target="tpu_custom_call" | custom-call | flops 427819008 | bytes 3538944 | tf_op jit(solution)/shard_map/pallas_call | solution.py:281
  28.2 0.5 %collective-permute-start.3 = (bf16[528,128]{1,0:T(8,128)(2,1)S(1)}, bf16[528,128]{1,0:T(8,128)(2,1)S(1)}, u32[]{:S(2)}, u32[]{:S(2)}) collective-permute-start(bf16[528,128]{1,0:T(8,128)(2,1)S(1)} %get-tuple-element.33), channel_id=1, source_target_pairs={{0,1},{1,0},{2,3},{3,2},{4,5},{5,4},{6,7},{7,6},{8,9},{9,8},{10,11... | collective-permute-start | bytes 405512 | tf_op jit(solution)/shard_map/ppermute | solution.py:276
  28.7 1.5 %collective-permute-start.4 = (bf16[528,128]{1,0:T(8,128)(2,1)S(1)}, bf16[528,128]{1,0:T(8,128)(2,1)S(1)}, u32[]{:S(2)}, u32[]{:S(2)}) collective-permute-start(bf16[528,128]{1,0:T(8,128)(2,1)S(1)} %get-tuple-element.34), channel_id=1, source_target_pairs={{0,2},{1,3},{2,0},{3,1},{4,6},{5,7},{6,4},{7,5},{8,10},{9,11},{10,... | collective-permute-start | bytes 405512 | tf_op jit(solution)/shard_map/ppermute | solution.py:276
  30.2 0.0 collective-permute-start.5
  30.2 1.4 %collective-permute-start.11 = (bf16[272,128]{1,0:T(8,128)(2,1)S(1)}, bf16[272,128]{1,0:T(8,128)(2,1)S(1)}, u32[]{:S(2)}, u32[]{:S(2)}) collective-permute-start(bf16[272,128]{1,0:T(8,128)(2,1)S(1)} %get-tuple-element.42), channel_id=1, source_target_pairs={{0,2},{1,3},{2,0},{3,1},{4,6},{5,7},{6,4},{7,5},{8,10},{9,11},{10,... | collective-permute-start | bytes 208904 | tf_op jit(solution)/shard_map/ppermute | solution.py:276
  31.7 0.0 collective-permute-done.10.refs_5_
  31.7 0.6 %collective-permute-start.12 = (bf16[272,128]{1,0:T(8,128)(2,1)S(1)}, bf16[272,128]{1,0:T(8,128)(2,1)S(1)}, u32[]{:S(2)}, u32[]{:S(2)}) collective-permute-start(bf16[272,128]{1,0:T(8,128)(2,1)S(1)} %get-tuple-element.43), channel_id=1, source_target_pairs={{0,3},{1,2},{2,1},{3,0},{4,7},{5,6},{6,5},{7,4},{8,11},{9,10},{10,... | collective-permute-start | bytes 208904 | tf_op jit(solution)/shard_map/ppermute | solution.py:276
  32.2 7.2 %collective-permute-done.11.refs_6_ = bf16[272,128]{1,0:T(8,128)(2,1)S(1)} collective-permute-done((bf16[272,128]{1,0:T(8,128)(2,1)S(1)}, bf16[272,128]{1,0:T(8,128)(2,1)S(1)}, u32[]{:S(2)}, u32[]{:S(2)}) %collective-permute-start.11) | collective-permute-done | bytes 69664 | tf_op jit(solution)/shard_map/ppermute | solution.py:276
  39.4 0.0 collective-permute-done.12.refs_7_
  39.4 0.0 collective-permute-done.3.refs_1_
  39.4 0.0 collective-permute-done.4.refs_2_
  39.4 0.0 collective-permute-done.5.refs_3_
  39.4 0.0 copy-done
  39.4 0.7 %shard_map.77 = (bf16[8,80,128]{2,1,0:T(8,128)(2,1)S(1)}, f32[256,128]{1,0:T(8,128)S(1)}, f32[4,16,128]{2,1,0:T(8,128)S(1)}) custom-call(bf16[16,512,128]{2,1,0:T(8,128)(2,1)S(1)} %copy-done, bf16[528,128]{1,0:T(8,128)(2,1)S(1)} %get-tuple-element.32.refs_0_, bf16[528,128]{1,0:T(8,128)(2,1)S(1)} %collective-permute-done.3.refs_1_, ...), custom_call_target="tpu_custom_call" | custom-call | tf_op jit(solution)/shard_map/pallas_call | solution.py:281
  40.2 11.7 %all_to_all.5.back_ref = bf16[8,80,128]{2,1,0:T(8,128)(2,1)S(1)} all-to-all(bf16[8,80,128]{2,1,0:T(8,128)(2,1)S(1)} %get-tuple-element.44), channel_id=1, replica_groups=mesh['dp'=8,'sub'=4] {'dp'}, dimensions={0} | all-to-all | bytes 327680 | tf_op jit(solution)/shard_map/all_to_all | solution.py:402
  51.9 1.7 %shard_map.78 = bf16[4,16,128]{2,1,0:T(8,128)(2,1)} custom-call(bf16[8,80,128]{2,1,0:T(8,128)(2,1)S(1)} %all_to_all.5.back_ref, f32[256,128]{1,0:T(8,128)S(1)} %get-tuple-element.45.own_ref, f32[4,16,128]{2,1,0:T(8,128)S(1)} %get-tuple-element.46.side_ref), custom_call_target="tpu_custom_call" | custom-call | tf_op jit(solution)/shard_map/pallas_call | solution.py:281
Async XLA Ops:
  0.0 21.7 %copy-start.1 = (s32[1,1,8]{2,1,0:T(1,128)S(1)}, s32[1,1,8]{2,1,0:T(1,128)}, u32[]{:S(2)}) copy-start(s32[1,1,8]{2,1,0:T(1,128)} %param.11) | copy-start | bytes 100
  1.2 8.9 %collective-permute-start.6 = (bf16[288,128]{1,0:T(8,128)(2,1)S(1)}, bf16[288,128]{1,0:T(8,128)(2,1)S(1)}, u32[]{:S(2)}, u32[]{:S(2)}) collective-permute-start(bf16[288,128]{1,0:T(8,128)(2,1)S(1)} %get-tuple-element.36), channel_id=1, source_target_pairs={{0,16},{4,20},{8,24},{12,28},{16,0},{20,4},{24,8},{28,12},{1,17},{... | collective-permute-start | bytes 221192 | tf_op jit(solution)/shard_map/ppermute | solution.py:276
  5.3 9.3 %collective-permute-start.7 = (bf16[288,128]{1,0:T(8,128)(2,1)S(1)}, bf16[288,128]{1,0:T(8,128)(2,1)S(1)}, u32[]{:S(2)}, u32[]{:S(2)}) collective-permute-start(bf16[288,128]{1,0:T(8,128)(2,1)S(1)} %get-tuple-element.37), channel_id=1, source_target_pairs={{0,20},{4,16},{8,28},{12,24},{16,4},{20,0},{24,12},{28,8},{1,21},{... | collective-permute-start | bytes 221192 | tf_op jit(solution)/shard_map/ppermute | solution.py:276
  6.6 18.6 %collective-permute-start = (bf16[288,128]{1,0:T(8,128)(2,1)S(1)}, bf16[288,128]{1,0:T(8,128)(2,1)S(1)}, u32[]{:S(2)}, u32[]{:S(2)}) collective-permute-start(bf16[288,128]{1,0:T(8,128)(2,1)S(1)} %get-tuple-element.29), channel_id=1, source_target_pairs={{0,4},{4,0},{8,12},{12,8},{16,20},{20,16},{24,28},{28,24},{1,5},{5... | collective-permute-start | bytes 221192 | tf_op jit(solution)/shard_map/ppermute | solution.py:276
  6.8 18.4 %collective-permute-start.1 = (bf16[288,128]{1,0:T(8,128)(2,1)S(1)}, bf16[288,128]{1,0:T(8,128)(2,1)S(1)}, u32[]{:S(2)}, u32[]{:S(2)}) collective-permute-start(bf16[288,128]{1,0:T(8,128)(2,1)S(1)} %get-tuple-element.30), channel_id=1, source_target_pairs={{0,8},{4,12},{8,0},{12,4},{16,24},{20,28},{24,16},{28,20},{1,9},{5... | collective-permute-start | bytes 221192 | tf_op jit(solution)/shard_map/ppermute | solution.py:276
  8.7 16.6 %collective-permute-start.2 = (bf16[288,128]{1,0:T(8,128)(2,1)S(1)}, bf16[288,128]{1,0:T(8,128)(2,1)S(1)}, u32[]{:S(2)}, u32[]{:S(2)}) collective-permute-start(bf16[288,128]{1,0:T(8,128)(2,1)S(1)} %get-tuple-element.31), channel_id=1, source_target_pairs={{0,12},{4,8},{8,4},{12,0},{16,28},{20,24},{24,20},{28,16},{1,13},{... | collective-permute-start | bytes 221192 | tf_op jit(solution)/shard_map/ppermute | solution.py:276
  10.1 11.2 %collective-permute-start.8 = (bf16[288,128]{1,0:T(8,128)(2,1)S(1)}, bf16[288,128]{1,0:T(8,128)(2,1)S(1)}, u32[]{:S(2)}, u32[]{:S(2)}) collective-permute-start(bf16[288,128]{1,0:T(8,128)(2,1)S(1)} %get-tuple-element.38), channel_id=1, source_target_pairs={{0,24},{4,28},{8,16},{12,20},{16,8},{20,12},{24,0},{28,4},{1,25},{... | collective-permute-start | bytes 221192 | tf_op jit(solution)/shard_map/ppermute | solution.py:276
  14.6 7.1 %collective-permute-start.9 = (bf16[288,128]{1,0:T(8,128)(2,1)S(1)}, bf16[288,128]{1,0:T(8,128)(2,1)S(1)}, u32[]{:S(2)}, u32[]{:S(2)}) collective-permute-start(bf16[288,128]{1,0:T(8,128)(2,1)S(1)} %get-tuple-element.39), channel_id=1, source_target_pairs={{0,28},{4,24},{8,20},{12,16},{16,12},{20,8},{24,4},{28,0},{1,29},{... | collective-permute-start | bytes 221192 | tf_op jit(solution)/shard_map/ppermute | solution.py:276
  21.7 17.8 %copy-start = (bf16[16,512,128]{2,1,0:T(8,128)(2,1)S(1)}, bf16[16,512,128]{2,1,0:T(8,128)(2,1)}, u32[]{:S(2)}) copy-start(bf16[16,512,128]{2,1,0:T(8,128)(2,1)} %value_ref.1) | copy-start | bytes 6291460
  25.1 6.5 %collective-permute-start.10 = (bf16[272,128]{1,0:T(8,128)(2,1)S(1)}, bf16[272,128]{1,0:T(8,128)(2,1)S(1)}, u32[]{:S(2)}, u32[]{:S(2)}) collective-permute-start(bf16[272,128]{1,0:T(8,128)(2,1)S(1)} %get-tuple-element.41), channel_id=1, source_target_pairs={{0,1},{1,0},{2,3},{3,2},{4,5},{5,4},{6,7},{7,6},{8,9},{9,8},{10,11... | collective-permute-start | bytes 208904 | tf_op jit(solution)/shard_map/ppermute | solution.py:276
  28.2 11.2 %collective-permute-start.3 = (bf16[528,128]{1,0:T(8,128)(2,1)S(1)}, bf16[528,128]{1,0:T(8,128)(2,1)S(1)}, u32[]{:S(2)}, u32[]{:S(2)}) collective-permute-start(bf16[528,128]{1,0:T(8,128)(2,1)S(1)} %get-tuple-element.33), channel_id=1, source_target_pairs={{0,1},{1,0},{2,3},{3,2},{4,5},{5,4},{6,7},{7,6},{8,9},{9,8},{10,11... | collective-permute-start | bytes 405512 | tf_op jit(solution)/shard_map/ppermute | solution.py:276
  28.7 10.7 %collective-permute-start.4 = (bf16[528,128]{1,0:T(8,128)(2,1)S(1)}, bf16[528,128]{1,0:T(8,128)(2,1)S(1)}, u32[]{:S(2)}, u32[]{:S(2)}) collective-permute-start(bf16[528,128]{1,0:T(8,128)(2,1)S(1)} %get-tuple-element.34), channel_id=1, source_target_pairs={{0,2},{1,3},{2,0},{3,1},{4,6},{5,7},{6,4},{7,5},{8,10},{9,11},{10,... | collective-permute-start | bytes 405512 | tf_op jit(solution)/shard_map/ppermute | solution.py:276
  30.2 9.2 %collective-permute-start.5 = (bf16[528,128]{1,0:T(8,128)(2,1)S(1)}, bf16[528,128]{1,0:T(8,128)(2,1)S(1)}, u32[]{:S(2)}, u32[]{:S(2)}) collective-permute-start(bf16[528,128]{1,0:T(8,128)(2,1)S(1)} %get-tuple-element.35), channel_id=1, source_target_pairs={{0,3},{1,2},{2,1},{3,0},{4,7},{5,6},{6,5},{7,4},{8,11},{9,10},{10,... | collective-permute-start | bytes 405512 | tf_op jit(solution)/shard_map/ppermute | solution.py:276
  30.2 9.2 %collective-permute-start.11 = (bf16[272,128]{1,0:T(8,128)(2,1)S(1)}, bf16[272,128]{1,0:T(8,128)(2,1)S(1)}, u32[]{:S(2)}, u32[]{:S(2)}) collective-permute-start(bf16[272,128]{1,0:T(8,128)(2,1)S(1)} %get-tuple-element.42), channel_id=1, source_target_pairs={{0,2},{1,3},{2,0},{3,1},{4,6},{5,7},{6,4},{7,5},{8,10},{9,11},{10,... | collective-permute-start | bytes 208904 | tf_op jit(solution)/shard_map/ppermute | solution.py:276
  31.7 7.8 %collective-permute-start.12 = (bf16[272,128]{1,0:T(8,128)(2,1)S(1)}, bf16[272,128]{1,0:T(8,128)(2,1)S(1)}, u32[]{:S(2)}, u32[]{:S(2)}) collective-permute-start(bf16[272,128]{1,0:T(8,128)(2,1)S(1)} %get-tuple-element.43), channel_id=1, source_target_pairs={{0,3},{1,2},{2,1},{3,0},{4,7},{5,6},{6,5},{7,4},{8,11},{9,10},{10,... | collective-permute-start | bytes 208904 | tf_op jit(solution)/shard_map/ppermute | solution.py:276

commit v2 on v1

--- a/solution.py
+++ b/solution.py
@@ -96,29 +96,26 @@
         stage[i, pl.ds(slot, heads, stride=rows), :] = partial[:, i * LANES:(i + 1) * LANES]
 
 
-def write_messages(stage, side, rows, outs, part, other=None, taken=0):
+def write_messages(stage, side, rows, outs, part):
     me = lax.axis_index("sub")
     for k, out in enumerate(outs):
         seat = me ^ k
         start = pl.multiple_of(seat * (part * rows), 8)
         for i in range(TILES):
             chunk = stage[i, pl.ds(start, part * rows), :]
-            if taken:
-                row = lax.broadcasted_iota(jnp.int32, chunk.shape, 0) % rows
-                chunk = jnp.where(row < taken, other[i, pl.ds(start, part * rows), :], chunk)
             out[i * part * rows:(i + 1) * part * rows, :] = chunk.astype(jnp.bfloat16)
         side_start = pl.multiple_of(seat * part, 8)
         out[TILES * part * rows:, :] = side[pl.ds(side_start, part), :].astype(jnp.bfloat16)
 
 
-def own_kernel(rows, plan_hbm, own_len_hbm, host_len_hbm, query_hbm, own_hbm, host_ref, cache_ref, stage, table_ref,
-               plan_ref, own_len_ref, host_len_ref, query_ref, own_ref, first_sems, sems):
+def own_kernel(rows, n_sub, plan_hbm, own_len_hbm, query_hbm, own_hbm, host_ref, cache_ref, self_ref, *refs):
+    outs, (plan_ref, own_len_ref, query_ref, own_ref, stage, side, first_sems, sems) = refs[:n_sub], refs[n_sub:]
     me = lax.axis_index("dp")
     groups = host_ref.shape[0]
     firsts = []
     for i, (source, target) in enumerate((
         (query_hbm, query_ref), (own_hbm, own_ref), (plan_hbm, plan_ref),
-        (own_len_hbm, own_len_ref), (host_len_hbm, host_len_ref),
+        (own_len_hbm, own_len_ref),
     )):
         firsts.append(pltpu.make_async_copy(source, target, first_sems.at[i]))
         firsts[i].start()
@@ -136,33 +133,32 @@
         partial, lse = attend(query[:, :DL], query[:, DL:], own_ref.at[r], own_len_ref[r])
         put_slot(stage, r, rows, partial)
         table = put_lane(table, r, lse)
-    copies[0].wait()
-    query = query_ref[plan_ref[me]]
-    partial, lse = attend(query[:, :DL], query[:, DL:], cache_ref.at[me], host_len_ref[me])
-    put_slot(stage, requests, rows, partial)
-    table = put_lane(table, requests, lse)
+    self_ref[...] = query_ref[plan_ref[me]]
+    table = split_three(table)
     for p in range(groups):
         table = put_lane(table, PLAN_LANE + p, plan_ref[p].astype(jnp.float32))
-    table_ref[...] = table
-    for copy in copies[1:]:
+    side[...] = table
+    write_messages(stage, side, rows, outs, heads // n_sub)
+    for copy in copies:
         copy.wait()
 
 
-def near_kernel(near, requests, rows, n_sub, host_len_ref, host_ref, own_stage, table_ref, *refs):
+def near_kernel(near, rows, n_sub, host_len_ref, host_ref, self_ref, *refs):
     packed, outs, (stage, side) = refs[: near - 1], refs[near - 1: near - 1 + n_sub], refs[near - 1 + n_sub:]
     me = lax.axis_index("dp")
     heads = side.shape[0]
-    table = table_ref[...]
-    lane = lane_index(table.shape)
-    for k in range(1, near):
+    table = jnp.zeros((heads, LANES), jnp.float32)
+    for k in range(near):
         g = me ^ k
-        latent, rotary = unpack_query(packed[k - 1], heads)
+        if k == 0:
+            latent, rotary = self_ref[:, :DL], self_ref[:, DL:]
+        else:
+            latent, rotary = unpack_query(packed[k - 1], heads)
         partial, lse = attend(latent, rotary, host_ref.at[g], host_len_ref[g])
-        put_slot(stage, requests + k, rows, partial)
-        table = put_lane(table, requests + k, lse)
-    pieces = split_three(jnp.where(lane < PIECE, table, 0.0))
-    side[...] = jnp.where(lane < PLAN_LANE, pieces, table)
-    write_messages(stage, side, rows, outs, heads // n_sub, own_stage, requests + 1)
+        put_slot(stage, k, rows, partial)
+        table = put_lane(table, k, lse)
+    side[...] = split_three(table)
+    write_messages(stage, side, rows, outs, heads // n_sub)
 
 
 def far_kernel(near, rows, n_sub, host_len_ref, host_ref, *refs):
@@ -184,49 +180,52 @@
     write_messages(stage, side, rows, outs, heads // n_sub)
 
 
-def lift_kernel(near, requests, near_rows, far_rows, n_sub, groups, value_ref, *refs):
-    near_in, far_in = refs[:n_sub], refs[n_sub: 2 * n_sub]
-    out, own_out, own_side, lhs, lifted = refs[2 * n_sub:]
+def lift_kernel(near, chunk_rows, n_sub, groups, value_ref, *refs):
+    chunks = len(chunk_rows)
+    sources = [refs[c * n_sub:(c + 1) * n_sub] for c in range(chunks)]
+    out, own_out, own_side, lhs, lifted = refs[chunks * n_sub:]
     me = lax.axis_index("dp")
     part = value_ref.shape[0]
-    near_block, far_block = max(near_rows, 8), max(far_rows, 8)
     seats = n_sub * part
+    blocks = [max(rows, 8) for rows in chunk_rows]
     for h in range(part):
         offset = 0
-        for sources, rows, block in ((near_in, near_rows, near_block), (far_in, far_rows, far_block)):
+        for refs_of, rows, block in zip(sources, chunk_rows, blocks):
             start = h * rows // block * block
-            for source in sources:
+            for source in refs_of:
                 for i in range(TILES):
                     base = i * part * rows + start
                     lhs[h, offset: offset + block, i * LANES:(i + 1) * LANES] = source[base: base + block, :]
                 offset += block
         result = jnp.dot(lhs[h], value_ref[h], preferred_element_type=jnp.float32)
-        for s in range(n_sub):
-            base = s * near_block
-            lifted[pl.ds(s * part + h, near_block, stride=seats), :] = result[base: base + near_block]
-            base = n_sub * near_block + s * far_block
-            piece = result[base: base + far_block]
-            skip = h * far_rows % far_block
-            if skip:
-                piece = pltpu.roll(piece, far_block - skip, 0)
-            lifted[pl.ds(near_block * seats + s * part + h, far_block, stride=seats), :] = piece
-    side_near = [ref[TILES * part * near_rows:, :].astype(jnp.float32) for ref in near_in]
-    side_far = [ref[TILES * part * far_rows:, :].astype(jnp.float32) for ref in far_in]
+        offset, slot = 0, 0
+        for rows, block in zip(chunk_rows, blocks):
+            skip = h * rows % block
+            for s in range(n_sub):
+                piece = result[offset: offset + block]
+                if skip:
+                    piece = pltpu.roll(piece, block - skip, 0)
+                lifted[pl.ds(slot * seats + s * part + h, block, stride=seats), :] = piece
+                offset += block
+            slot += block
+    sides = [
+        [ref[TILES * part * rows:, :].astype(jnp.float32) for ref in refs_of]
+        for refs_of, rows in zip(sources, chunk_rows)
+    ]
     lane = lane_index((part, LANES))
     for k in range(groups):
-        g = me ^ k
-        row = requests + k if k < near else k - near
-        first = (row if k < near else near_block + row) * seats
-        out[g, :seats, :] = lifted[first: first + seats, :].astype(jnp.bfloat16)
+        chunk, row = (1, k) if k < near else (2, k - near)
+        first = (sum(blocks[:chunk]) + row) * seats
+        out[me ^ k, :seats, :] = lifted[first: first + seats, :].astype(jnp.bfloat16)
         tile = jnp.zeros((part, LANES), jnp.float32)
         for s in range(n_sub):
-            source = side_near[s] if k < near else side_far[s]
+            source = sides[chunk][s]
             moved = pltpu.roll(source, (s - row) % LANES, 1) if s != row else source
             tile = jnp.where((lane % PIECE == s) & (lane < 3 * PIECE), moved, tile)
-        out[g, seats:, :] = tile.astype(jnp.bfloat16)
-    own_out[...] = lifted[: requests * seats, :]
+        out[me ^ k, seats:, :] = tile.astype(jnp.bfloat16)
+    own_out[...] = lifted[: own_out.shape[0], :]
     for s in range(n_sub):
-        own_side[s] = side_near[s]
+        own_side[s] = sides[0][s]
 
 
 def finish_kernel(requests, n_sub, groups, back_ref, own_ref, side_ref, out_ref):
@@ -295,6 +294,10 @@
     return pltpu.with_memory_space_constraint(array, pltpu.HBM)
 
 
+def padded_rows(count):
+    return count if count in (1, 2, 4) else -(-count // 8) * 8
+
+
 def near_count(groups):
     return min(4, groups)
 
@@ -306,8 +309,7 @@
     slot_tokens = host_cache.shape[3]
     near = near_count(groups)
     far = groups - near
-    near_rows = requests + near
-    far_rows = far if far in (1, 2, 4) else -(-far // 8) * 8
+    own_rows, near_rows, far_rows = padded_rows(requests), padded_rows(near), padded_rows(far)
     plan = page_plan.reshape(groups)
     lengths = host_len.reshape(groups)
     own_lengths = own_len.reshape(requests)
@@ -340,34 +342,33 @@
             transcendentals=slots * heads * slot_tokens,
         )
 
-    cache, own_stage, table = call(
-        functools.partial(own_kernel, near_rows),
+    cache, self_query, *own_out = call(
+        functools.partial(own_kernel, own_rows, n_sub),
         [
             jax.ShapeDtypeStruct(host_keys.shape, host_keys.dtype),
-            jax.ShapeDtypeStruct(stage_shape(near_rows), jnp.float32),
-            jax.ShapeDtypeStruct((heads, LANES), jnp.float32),
-        ],
-        [HBM] * 6,
+            jax.ShapeDtypeStruct((heads, width), queries.dtype),
+        ] + [message(own_rows)] * n_sub,
+        [HBM] * 5,
         [
             pltpu.SMEM(plan.shape, plan.dtype),
             pltpu.SMEM(own_lengths.shape, own_lengths.dtype),
-            pltpu.SMEM(lengths.shape, lengths.dtype),
             pltpu.VMEM(queries.shape, queries.dtype),
             pltpu.VMEM(own_keys.shape, own_keys.dtype),
-            pltpu.SemaphoreType.DMA((5,)),
+        ] + stages(own_rows) + [
+            pltpu.SemaphoreType.DMA((4,)),
             pltpu.SemaphoreType.DMA((groups,)),
         ],
         limit=OWN_LIMIT,
         cost=cost(groups),
-    )(*[in_hbm(x) for x in (plan, own_lengths, lengths, queries, own_keys, host_keys)])
+    )(*[in_hbm(x) for x in (plan, own_lengths, queries, own_keys, host_keys)])
     near_out = call(
-        functools.partial(near_kernel, near, requests, near_rows, n_sub),
+        functools.partial(near_kernel, near, near_rows, n_sub),
         [message(near_rows)] * n_sub,
-        [SMEM] + [VMEM] * (3 + near - 1),
+        [SMEM] + [VMEM] * (2 + near - 1),
         stages(near_rows),
         limit=KERNEL_LIMIT,
-        cost=cost(near - 1),
-    )(lengths, cache, own_stage, table, *[received[k] for k in range(1, near)])
+        cost=cost(near),
+    )(lengths, cache, self_query, *[received[k] for k in range(1, near)])
     far_out = call(
         functools.partial(far_kernel, near, far_rows, n_sub),
         [message(far_rows)] * n_sub,
@@ -377,28 +378,28 @@
         cost=cost(far),
     )(lengths, cache, *[received[k] for k in range(near, groups)])
     sub_order = [k for k in range(2, n_sub)] + [1]
-    near_in, far_in = {0: near_out[0]}, {0: far_out[0]}
-    for k in sub_order:
-        near_in[k] = exchange(near_out[k], "sub", k)
-    for k in sub_order:
-        far_in[k] = exchange(far_out[k], "sub", k)
-
-    near_block, far_block = max(near_rows, 8), max(far_rows, 8)
+    arrived = []
+    for messages in (own_out, near_out, far_out):
+        moved = {k: exchange(messages[k], "sub", k) for k in sub_order}
+        arrived += [messages[0]] + [moved[k] for k in range(1, n_sub)]
+
+    chunk_rows = (own_rows, near_rows, far_rows)
+    slots = sum(max(rows, 8) for rows in chunk_rows)
     seats = n_sub * part
     back, own, side = call(
-        functools.partial(lift_kernel, near, requests, near_rows, far_rows, n_sub, groups),
+        functools.partial(lift_kernel, near, chunk_rows, n_sub, groups),
         [
             jax.ShapeDtypeStruct((groups, seats + part, LANES), jnp.bfloat16),
             jax.ShapeDtypeStruct((requests * seats, LANES), jnp.float32),
             jax.ShapeDtypeStruct((n_sub, part, LANES), jnp.float32),
         ],
-        [VMEM] * (1 + 2 * n_sub),
+        [VMEM] * (1 + 3 * n_sub),
         [
-            pltpu.VMEM((part, n_sub * (near_block + far_block), DL), jnp.bfloat16),
-            pltpu.VMEM(((near_block + far_block) * seats, LANES), jnp.float32),
+            pltpu.VMEM((part, n_sub * slots, DL), jnp.bfloat16),
+            pltpu.VMEM((slots * seats, LANES), jnp.float32),
         ],
         limit=12 << 20,
-    )(value_up, *[near_in[k] for k in range(n_sub)], *[far_in[k] for k in range(n_sub)])
+    )(value_up, *arrived)
     back = lax.all_to_all(back, "dp", split_axis=0, concat_axis=0, tiled=True)
     return call(
         functools.partial(finish_kernel, requests, n_sub, groups),

time: 53.8 us -> 52.4 us (0.974)
  waiting for transfers between devices: 7.58 us -> 5.24 us
  blocking collectives: 11.7 us -> 13.4 us
  starting transfers between devices: 20 us -> 18.6 us
  Pallas kernels: 14.2 us -> 14.9 us
    ppermute x13 -> x16, waiting for transfers between devices: 7.58 us -> 5.24 us  [exchange(): return lax.ppermute(array, axis, [(i, i ^ k) for i in range(size)])]
    all_to_all x1, blocking collectives: 11.7 us -> 13.4 us  [local(): back = lax.all_to_all(back, 'dp', split_axis=0, concat_axis=0, tiled=True)]
    ppermute x13 -> x16, starting transfers between devices: 20 us -> 18.6 us  [exchange(): return lax.ppermute(array, axis, [(i, i ^ k) for i in range(size)])]
    pallas_call x6, Pallas kernels: 14.2 us -> 14.9 us  [run(): pl.pallas_call(kernel, out_shape=outs, in_specs=in_specs, out_specs=jax.t...]
  transfers between devices with their start and end apart: 13 -> 16, of which waited for: 2 -> 3; matrix products, arithmetic and copies ran while one was open for 0% -> 0% of each run, Pallas kernels for 20% -> 21%
where the time goes in v2:
time: 52.4 us; the launch traced here: 52.3 us
  starting transfers between devices  18.6 us (35%)
  Pallas kernels  14.9 us (28%)
  blocking collectives  13.4 us (26%)
  waiting for transfers between devices  5.24 us (10%)
    ppermute x16, starting transfers between devices, exchange(): return lax.ppermute(array, axis, [(i, i ^ k) for i in range(size)])  18.6 us
    pallas_call x6, Pallas kernels, run(): pl.pallas_call(kernel, out_shape=outs, in_specs=in_specs, out_specs=jax.t...  14.9 us
    all_to_all x1, blocking collectives, local(): back = lax.all_to_all(back, 'dp', split_axis=0, concat_axis=0, tiled=True)  13.4 us
    ppermute x16, waiting for transfers between devices, exchange(): return lax.ppermute(array, axis, [(i, i ^ k) for i in range(size)])  5.24 us
  transfers between devices with their start and end apart: 16, of which 3 were waited for; matrix products, arithmetic and copies ran while one was open for 0% of the time, Pallas kernels for 21%

profile of v2, /device:TPU:0, one launch (start us, length us, event | category | flops | bytes accessed | tf_op | source)
XLA Modules:
  0.0 52.3 jit_solution(17149891307718046550)
XLA Ops:
  0.0 0.0 copy-start.1
  0.0 1.2 %shard_map.74 = (bf16[288,128]{1,0:T(8,128)(2,1)S(1)}, bf16[288,128]{1,0:T(8,128)(2,1)S(1)}, bf16[288,128]{1,0:T(8,128)(2,1)S(1)}, bf16[288,128]{1,0:T(8,128)(2,...) custom-call(s32[8]{0:T(128)} %bitcast.11, ...), custom_call_target="tpu_custom_call" | custom-call | tf_op jit(solution)/shard_map/pallas_call | solution.py:280
  1.2 3.1 %collective-permute-start.3 = (bf16[288,128]{1,0:T(8,128)(2,1)S(1)}, bf16[288,128]{1,0:T(8,128)(2,1)S(1)}, u32[]{:S(2)}, u32[]{:S(2)}) collective-permute-start(bf16[288,128]{1,0:T(8,128)(2,1)S(1)} %get-tuple-element.35), channel_id=1, source_target_pairs={{0,4},{4,0},{8,12},{12,8},{16,20},{20,16},{24,28},{28,24},{1,5},{5... | collective-permute-start | bytes 221192 | tf_op jit(solution)/shard_map/ppermute | solution.py:275
  4.2 1.6 %collective-permute-start.4 = (bf16[288,128]{1,0:T(8,128)(2,1)S(1)}, bf16[288,128]{1,0:T(8,128)(2,1)S(1)}, u32[]{:S(2)}, u32[]{:S(2)}) collective-permute-start(bf16[288,128]{1,0:T(8,128)(2,1)S(1)} %get-tuple-element.36), channel_id=1, source_target_pairs={{0,8},{4,12},{8,0},{12,4},{16,24},{20,28},{24,16},{28,20},{1,9},{5... | collective-permute-start | bytes 221192 | tf_op jit(solution)/shard_map/ppermute | solution.py:275
  5.8 0.0 collective-permute-start.5
  5.8 3.0 %collective-permute-start.9 = (bf16[288,128]{1,0:T(8,128)(2,1)S(1)}, bf16[288,128]{1,0:T(8,128)(2,1)S(1)}, u32[]{:S(2)}, u32[]{:S(2)}) collective-permute-start(bf16[288,128]{1,0:T(8,128)(2,1)S(1)} %get-tuple-element.42), channel_id=1, source_target_pairs={{0,16},{4,20},{8,24},{12,28},{16,0},{20,4},{24,8},{28,12},{1,17},{... | collective-permute-start | bytes 221192 | tf_op jit(solution)/shard_map/ppermute | solution.py:275
  8.8 1.3 %collective-permute-start.10 = (bf16[288,128]{1,0:T(8,128)(2,1)S(1)}, bf16[288,128]{1,0:T(8,128)(2,1)S(1)}, u32[]{:S(2)}, u32[]{:S(2)}) collective-permute-start(bf16[288,128]{1,0:T(8,128)(2,1)S(1)} %get-tuple-element.43), channel_id=1, source_target_pairs={{0,20},{4,16},{8,28},{12,24},{16,4},{20,0},{24,12},{28,8},{1,21},{... | collective-permute-start | bytes 221192 | tf_op jit(solution)/shard_map/ppermute | solution.py:275
  10.1 0.0 collective-permute-done.3.refs_0_
  10.1 3.6 %collective-permute-start.11 = (bf16[288,128]{1,0:T(8,128)(2,1)S(1)}, bf16[288,128]{1,0:T(8,128)(2,1)S(1)}, u32[]{:S(2)}, u32[]{:S(2)}) collective-permute-start(bf16[288,128]{1,0:T(8,128)(2,1)S(1)} %get-tuple-element.44), channel_id=1, source_target_pairs={{0,24},{4,28},{8,16},{12,20},{16,8},{20,12},{24,0},{28,4},{1,25},{... | collective-permute-start | bytes 221192 | tf_op jit(solution)/shard_map/ppermute | solution.py:275
  13.7 0.0 collective-permute-done.4.refs_1_
  13.7 0.0 collective-permute-start.12
  13.7 4.3 %shard_map.73 = (bf16[8,576,1024]{2,1,0:T(8,128)(2,1)S(1)}, bf16[64,576]{1,0:T(8,128)(2,1)S(1)}, bf16[272,128]{1,0:T(8,128)(2,1)S(1)}, bf16[272,128]{1,0:T(8,128...) custom-call(s32[8]{0:T(128)} %bitcast.12, s32[4]{0:T(128)} %bitcast.13, ...), custom_call_target="tpu_custom_call" | custom-call | flops 1140850688 | bytes 9437184 | tf_op jit(solution)/shard_map/pallas_call | solution.py:280
  18.0 0.0 collective-permute-done.5.refs_2_
  18.0 0.1 collective-permute-start
  18.1 0.0 copy-done.1
  18.1 0.0 copy-start
  18.1 3.4 %shard_map.75 = (bf16[272,128]{1,0:T(8,128)(2,1)S(1)}, bf16[272,128]{1,0:T(8,128)(2,1)S(1)}, bf16[272,128]{1,0:T(8,128)(2,1)S(1)}, bf16[272,128]{1,0:T(8,128)(2,1)S(1)}) custom-call(s32[8]{0:T(128)S(1)} %bitcast.7, bf16[8,576,1024]{2,1,0:T(8,128)(2,1)S(1)} %get-tuple-element.33.host_ref, bf16[64,576]{1,0:T(8,128)(2,1)S(1)} %get-tuple-element.34.self_ref, ...), custom_call_target="tpu_custom_call" | custom-call | flops 570425344 | bytes 4718592 | tf_op jit(solution)/shard_map/pallas_call | solution.py:280
  21.5 0.0 collective-permute-done.9.refs_0_
  21.5 1.7 %collective-permute-start.1 = (bf16[272,128]{1,0:T(8,128)(2,1)S(1)}, bf16[272,128]{1,0:T(8,128)(2,1)S(1)}, u32[]{:S(2)}, u32[]{:S(2)}) collective-permute-start(bf16[272,128]{1,0:T(8,128)(2,1)S(1)} %get-tuple-element.31), channel_id=1, source_target_pairs={{0,2},{1,3},{2,0},{3,1},{4,6},{5,7},{6,4},{7,5},{8,10},{9,11},{10,... | collective-permute-start | bytes 208904 | tf_op jit(solution)/shard_map/ppermute | solution.py:275
  23.2 0.0 collective-permute-done.10.refs_1_
  23.2 0.2 collective-permute-start.2
  23.4 0.0 collective-permute-done.11.refs_2_
  23.4 0.3 collective-permute-start.6
  23.7 0.0 collective-permute-done.12.refs_3_
  23.7 1.6 %collective-permute-start.7 = (bf16[272,128]{1,0:T(8,128)(2,1)S(1)}, bf16[272,128]{1,0:T(8,128)(2,1)S(1)}, u32[]{:S(2)}, u32[]{:S(2)}) collective-permute-start(bf16[272,128]{1,0:T(8,128)(2,1)S(1)} %get-tuple-element.40), channel_id=1, source_target_pairs={{0,2},{1,3},{2,0},{3,1},{4,6},{5,7},{6,4},{7,5},{8,10},{9,11},{10,... | collective-permute-start | bytes 208904 | tf_op jit(solution)/shard_map/ppermute | solution.py:275
  25.4 3.5 %shard_map.76 = (bf16[272,128]{1,0:T(8,128)(2,1)S(1)}, bf16[272,128]{1,0:T(8,128)(2,1)S(1)}, bf16[272,128]{1,0:T(8,128)(2,1)S(1)}, bf16[272,128]{1,0:T(8,128)(2,1)S(1)}) custom-call(s32[8]{0:T(128)S(1)} %bitcast.8, bf16[8,576,1024]{2,1,0:T(8,128)(2,1)S(1)} %get-tuple-element.33.host_ref, bf16[288,128]{1,0:T(8,128)(2,1)S(1)} %collective-permute-done.9.refs_0_, ...), custom_call_target="tpu_custom_call" | custom-call | flops 570425344 | bytes 4718592 | tf_op jit(solution)/shard_map/pallas_call | solution.py:280
  28.9 0.0 collective-permute-done.refs_1_
  28.9 0.1 collective-permute-start.8
  28.9 0.0 collective-permute-done.1.refs_2_
  29.0 0.5 collective-permute-start.13
  29.4 0.0 collective-permute-done.2.refs_3_
  29.4 1.6 %collective-permute-start.14 = (bf16[272,128]{1,0:T(8,128)(2,1)S(1)}, bf16[272,128]{1,0:T(8,128)(2,1)S(1)}, u32[]{:S(2)}, u32[]{:S(2)}) collective-permute-start(bf16[272,128]{1,0:T(8,128)(2,1)S(1)} %get-tuple-element.48), channel_id=1, source_target_pairs={{0,2},{1,3},{2,0},{3,1},{4,6},{5,7},{6,4},{7,5},{8,10},{9,11},{10,... | collective-permute-start | bytes 208904 | tf_op jit(solution)/shard_map/ppermute | solution.py:275
  31.1 0.0 collective-permute-done.6.refs_5_
  31.1 0.0 collective-permute-start.15
  31.1 0.0 collective-permute-done.7.refs_6_
  31.1 2.2 %collective-permute-done.8.refs_7_ = bf16[272,128]{1,0:T(8,128)(2,1)S(1)} collective-permute-done((bf16[272,128]{1,0:T(8,128)(2,1)S(1)}, bf16[272,128]{1,0:T(8,128)(2,1)S(1)}, u32[]{:S(2)}, u32[]{:S(2)}) %collective-permute-start.8) | collective-permute-done | bytes 69664 | tf_op jit(solution)/shard_map/ppermute | solution.py:275
  33.3 0.0 collective-permute-done.13.refs_9_
  33.3 1.7 %collective-permute-done.14.refs_10_ = bf16[272,128]{1,0:T(8,128)(2,1)S(1)} collective-permute-done((bf16[272,128]{1,0:T(8,128)(2,1)S(1)}, bf16[272,128]{1,0:T(8,128)(2,1)S(1)}, u32[]{:S(2)}, u32[]{:S(2)}) %collective-permute-start.14) | collective-permute-done | bytes 69664 | tf_op jit(solution)/shard_map/ppermute | solution.py:275
  35.0 1.3 %collective-permute-done.15.refs_11_ = bf16[272,128]{1,0:T(8,128)(2,1)S(1)} collective-permute-done((bf16[272,128]{1,0:T(8,128)(2,1)S(1)}, bf16[272,128]{1,0:T(8,128)(2,1)S(1)}, u32[]{:S(2)}, u32[]{:S(2)}) %collective-permute-start.15) | collective-permute-done | bytes 69664 | tf_op jit(solution)/shard_map/ppermute | solution.py:275
  36.3 0.0 copy-done
  36.3 0.8 %shard_map.77 = (bf16[8,80,128]{2,1,0:T(8,128)(2,1)S(1)}, f32[256,128]{1,0:T(8,128)S(1)}, f32[4,16,128]{2,1,0:T(8,128)S(1)}) custom-call(bf16[16,512,128]{2,1,0:T(8,128)(2,1)S(1)} %copy-done, bf16[272,128]{1,0:T(8,128)(2,1)S(1)} %get-tuple-element.29.refs_0_, bf16[272,128]{1,0:T(8,128)(2,1)S(1)} %collective-permute-done.refs_1_, ...), custom_call_target="tpu_custom_call" | custom-call | tf_op jit(solution)/shard_map/pallas_call | solution.py:280
  37.2 13.4 %all_to_all.5.back_ref = bf16[8,80,128]{2,1,0:T(8,128)(2,1)S(1)} all-to-all(bf16[8,80,128]{2,1,0:T(8,128)(2,1)S(1)} %get-tuple-element.50), channel_id=1, replica_groups=mesh['dp'=8,'sub'=4] {'dp'}, dimensions={0} | all-to-all | bytes 327680 | tf_op jit(solution)/shard_map/all_to_all | solution.py:403
  50.6 1.7 %shard_map.78 = bf16[4,16,128]{2,1,0:T(8,128)(2,1)} custom-call(bf16[8,80,128]{2,1,0:T(8,128)(2,1)S(1)} %all_to_all.5.back_ref, f32[256,128]{1,0:T(8,128)S(1)} %get-tuple-element.51.own_ref, f32[4,16,128]{2,1,0:T(8,128)S(1)} %get-tuple-element.52.side_ref), custom_call_target="tpu_custom_call" | custom-call | tf_op jit(solution)/shard_map/pallas_call | solution.py:280
Async XLA Ops:
  0.0 18.1 %copy-start.1 = (s32[1,1,8]{2,1,0:T(1,128)S(1)}, s32[1,1,8]{2,1,0:T(1,128)}, u32[]{:S(2)}) copy-start(s32[1,1,8]{2,1,0:T(1,128)} %param.11) | copy-start | bytes 100
  1.2 8.9 %collective-permute-start.3 = (bf16[288,128]{1,0:T(8,128)(2,1)S(1)}, bf16[288,128]{1,0:T(8,128)(2,1)S(1)}, u32[]{:S(2)}, u32[]{:S(2)}) collective-permute-start(bf16[288,128]{1,0:T(8,128)(2,1)S(1)} %get-tuple-element.35), channel_id=1, source_target_pairs={{0,4},{4,0},{8,12},{12,8},{16,20},{20,16},{24,28},{28,24},{1,5},{5... | collective-permute-start | bytes 221192 | tf_op jit(solution)/shard_map/ppermute | solution.py:275
  4.2 9.5 %collective-permute-start.4 = (bf16[288,128]{1,0:T(8,128)(2,1)S(1)}, bf16[288,128]{1,0:T(8,128)(2,1)S(1)}, u32[]{:S(2)}, u32[]{:S(2)}) collective-permute-start(bf16[288,128]{1,0:T(8,128)(2,1)S(1)} %get-tuple-element.36), channel_id=1, source_target_pairs={{0,8},{4,12},{8,0},{12,4},{16,24},{20,28},{24,16},{28,20},{1,9},{5... | collective-permute-start | bytes 221192 | tf_op jit(solution)/shard_map/ppermute | solution.py:275
  5.8 12.2 %collective-permute-start.5 = (bf16[288,128]{1,0:T(8,128)(2,1)S(1)}, bf16[288,128]{1,0:T(8,128)(2,1)S(1)}, u32[]{:S(2)}, u32[]{:S(2)}) collective-permute-start(bf16[288,128]{1,0:T(8,128)(2,1)S(1)} %get-tuple-element.37), channel_id=1, source_target_pairs={{0,12},{4,8},{8,4},{12,0},{16,28},{20,24},{24,20},{28,16},{1,13},{... | collective-permute-start | bytes 221192 | tf_op jit(solution)/shard_map/ppermute | solution.py:275
  5.8 15.7 %collective-permute-start.9 = (bf16[288,128]{1,0:T(8,128)(2,1)S(1)}, bf16[288,128]{1,0:T(8,128)(2,1)S(1)}, u32[]{:S(2)}, u32[]{:S(2)}) collective-permute-start(bf16[288,128]{1,0:T(8,128)(2,1)S(1)} %get-tuple-element.42), channel_id=1, source_target_pairs={{0,16},{4,20},{8,24},{12,28},{16,0},{20,4},{24,8},{28,12},{1,17},{... | collective-permute-start | bytes 221192 | tf_op jit(solution)/shard_map/ppermute | solution.py:275
  8.8 14.4 %collective-permute-start.10 = (bf16[288,128]{1,0:T(8,128)(2,1)S(1)}, bf16[288,128]{1,0:T(8,128)(2,1)S(1)}, u32[]{:S(2)}, u32[]{:S(2)}) collective-permute-start(bf16[288,128]{1,0:T(8,128)(2,1)S(1)} %get-tuple-element.43), channel_id=1, source_target_pairs={{0,20},{4,16},{8,28},{12,24},{16,4},{20,0},{24,12},{28,8},{1,21},{... | collective-permute-start | bytes 221192 | tf_op jit(solution)/shard_map/ppermute | solution.py:275
  10.1 13.3 %collective-permute-start.11 = (bf16[288,128]{1,0:T(8,128)(2,1)S(1)}, bf16[288,128]{1,0:T(8,128)(2,1)S(1)}, u32[]{:S(2)}, u32[]{:S(2)}) collective-permute-start(bf16[288,128]{1,0:T(8,128)(2,1)S(1)} %get-tuple-element.44), channel_id=1, source_target_pairs={{0,24},{4,28},{8,16},{12,20},{16,8},{20,12},{24,0},{28,4},{1,25},{... | collective-permute-start | bytes 221192 | tf_op jit(solution)/shard_map/ppermute | solution.py:275
  13.7 10.0 %collective-permute-start.12 = (bf16[288,128]{1,0:T(8,128)(2,1)S(1)}, bf16[288,128]{1,0:T(8,128)(2,1)S(1)}, u32[]{:S(2)}, u32[]{:S(2)}) collective-permute-start(bf16[288,128]{1,0:T(8,128)(2,1)S(1)} %get-tuple-element.45), channel_id=1, source_target_pairs={{0,28},{4,24},{8,20},{12,16},{16,12},{20,8},{24,4},{28,0},{1,29},{... | collective-permute-start | bytes 221192 | tf_op jit(solution)/shard_map/ppermute | solution.py:275
  18.0 10.9 %collective-permute-start = (bf16[272,128]{1,0:T(8,128)(2,1)S(1)}, bf16[272,128]{1,0:T(8,128)(2,1)S(1)}, u32[]{:S(2)}, u32[]{:S(2)}) collective-permute-start(bf16[272,128]{1,0:T(8,128)(2,1)S(1)} %get-tuple-element.30), channel_id=1, source_target_pairs={{0,1},{1,0},{2,3},{3,2},{4,5},{5,4},{6,7},{7,6},{8,9},{9,8},{10,11... | collective-permute-start | bytes 208904 | tf_op jit(solution)/shard_map/ppermute | solution.py:275
  18.1 18.2 %copy-start = (bf16[16,512,128]{2,1,0:T(8,128)(2,1)S(1)}, bf16[16,512,128]{2,1,0:T(8,128)(2,1)}, u32[]{:S(2)}) copy-start(bf16[16,512,128]{2,1,0:T(8,128)(2,1)} %value_ref.1) | copy-start | bytes 6291460
  21.5 7.4 %collective-permute-start.1 = (bf16[272,128]{1,0:T(8,128)(2,1)S(1)}, bf16[272,128]{1,0:T(8,128)(2,1)S(1)}, u32[]{:S(2)}, u32[]{:S(2)}) collective-permute-start(bf16[272,128]{1,0:T(8,128)(2,1)S(1)} %get-tuple-element.31), channel_id=1, source_target_pairs={{0,2},{1,3},{2,0},{3,1},{4,6},{5,7},{6,4},{7,5},{8,10},{9,11},{10,... | collective-permute-start | bytes 208904 | tf_op jit(solution)/shard_map/ppermute | solution.py:275
  23.2 6.2 %collective-permute-start.2 = (bf16[272,128]{1,0:T(8,128)(2,1)S(1)}, bf16[272,128]{1,0:T(8,128)(2,1)S(1)}, u32[]{:S(2)}, u32[]{:S(2)}) collective-permute-start(bf16[272,128]{1,0:T(8,128)(2,1)S(1)} %get-tuple-element.32), channel_id=1, source_target_pairs={{0,3},{1,2},{2,1},{3,0},{4,7},{5,6},{6,5},{7,4},{8,11},{9,10},{10,... | collective-permute-start | bytes 208904 | tf_op jit(solution)/shard_map/ppermute | solution.py:275
  23.4 7.7 %collective-permute-start.6 = (bf16[272,128]{1,0:T(8,128)(2,1)S(1)}, bf16[272,128]{1,0:T(8,128)(2,1)S(1)}, u32[]{:S(2)}, u32[]{:S(2)}) collective-permute-start(bf16[272,128]{1,0:T(8,128)(2,1)S(1)} %get-tuple-element.39), channel_id=1, source_target_pairs={{0,1},{1,0},{2,3},{3,2},{4,5},{5,4},{6,7},{7,6},{8,9},{9,8},{10,11... | collective-permute-start | bytes 208904 | tf_op jit(solution)/shard_map/ppermute | solution.py:275
  23.7 7.4 %collective-permute-start.7 = (bf16[272,128]{1,0:T(8,128)(2,1)S(1)}, bf16[272,128]{1,0:T(8,128)(2,1)S(1)}, u32[]{:S(2)}, u32[]{:S(2)}) collective-permute-start(bf16[272,128]{1,0:T(8,128)(2,1)S(1)} %get-tuple-element.40), channel_id=1, source_target_pairs={{0,2},{1,3},{2,0},{3,1},{4,6},{5,7},{6,4},{7,5},{8,10},{9,11},{10,... | collective-permute-start | bytes 208904 | tf_op jit(solution)/shard_map/ppermute | solution.py:275
  28.9 4.5 %collective-permute-start.8 = (bf16[272,128]{1,0:T(8,128)(2,1)S(1)}, bf16[272,128]{1,0:T(8,128)(2,1)S(1)}, u32[]{:S(2)}, u32[]{:S(2)}) collective-permute-start(bf16[272,128]{1,0:T(8,128)(2,1)S(1)} %get-tuple-element.41), channel_id=1, source_target_pairs={{0,3},{1,2},{2,1},{3,0},{4,7},{5,6},{6,5},{7,4},{8,11},{9,10},{10,... | collective-permute-start | bytes 208904 | tf_op jit(solution)/shard_map/ppermute | solution.py:275
  29.0 4.4 %collective-permute-start.13 = (bf16[272,128]{1,0:T(8,128)(2,1)S(1)}, bf16[272,128]{1,0:T(8,128)(2,1)S(1)}, u32[]{:S(2)}, u32[]{:S(2)}) collective-permute-start(bf16[272,128]{1,0:T(8,128)(2,1)S(1)} %get-tuple-element.47), channel_id=1, source_target_pairs={{0,1},{1,0},{2,3},{3,2},{4,5},{5,4},{6,7},{7,6},{8,9},{9,8},{10,11... | collective-permute-start | bytes 208904 | tf_op jit(solution)/shard_map/ppermute | solution.py:275
  29.4 5.6 %collective-permute-start.14 = (bf16[272,128]{1,0:T(8,128)(2,1)S(1)}, bf16[272,128]{1,0:T(8,128)(2,1)S(1)}, u32[]{:S(2)}, u32[]{:S(2)}) collective-permute-start(bf16[272,128]{1,0:T(8,128)(2,1)S(1)} %get-tuple-element.48), channel_id=1, source_target_pairs={{0,2},{1,3},{2,0},{3,1},{4,6},{5,7},{6,4},{7,5},{8,10},{9,11},{10,... | collective-permute-start | bytes 208904 | tf_op jit(solution)/shard_map/ppermute | solution.py:275
  31.1 5.2 %collective-permute-start.15 = (bf16[272,128]{1,0:T(8,128)(2,1)S(1)}, bf16[272,128]{1,0:T(8,128)(2,1)S(1)}, u32[]{:S(2)}, u32[]{:S(2)}) collective-permute-start(bf16[272,128]{1,0:T(8,128)(2,1)S(1)} %get-tuple-element.49), channel_id=1, source_target_pairs={{0,3},{1,2},{2,1},{3,0},{4,7},{5,6},{6,5},{7,4},{8,11},{9,10},{10,... | collective-permute-start | bytes 208904 | tf_op jit(solution)/shard_map/ppermute | solution.py:275

commit v3 on v1

--- a/solution.py
+++ b/solution.py
@@ -295,6 +295,13 @@
     return pltpu.with_memory_space_constraint(array, pltpu.HBM)
 
 
+def start_order(groups):
+    near = near_count(groups)
+    far = list(range(near, groups))
+    half = len(far) // 2
+    return far[:half] + list(range(1, near)) + far[half:]
+
+
 def near_count(groups):
     return min(4, groups)
 
@@ -321,7 +328,7 @@
         [pltpu.SMEM(plan.shape, plan.dtype), pltpu.VMEM(queries.shape, queries.dtype), pltpu.SemaphoreType.DMA((2,))],
         limit=PACK_LIMIT,
     )(in_hbm(plan), in_hbm(queries))
-    order = list(range(near, groups)) + list(range(1, near))
+    order = start_order(groups)
     received = {k: exchange(outgoing[k - 1], "dp", k) for k in order}
 
     def message(rows):

time: 53.8 us -> 53.8 us (level)
  no operation moved by 1% of the time
where the time goes in v3:
time: 53.8 us; the launch traced here: 53.6 us
  starting transfers between devices  20 us (37%)
  Pallas kernels  14.2 us (26%)
  blocking collectives  11.7 us (22%)
  waiting for transfers between devices  7.58 us (14%)
    ppermute x13, starting transfers between devices, exchange(): return lax.ppermute(array, axis, [(i, i ^ k) for i in range(size)])  20 us
    pallas_call x6, Pallas kernels, run(): pl.pallas_call(kernel, out_shape=outs, in_specs=in_specs, out_specs=jax.t...  14.2 us
    all_to_all x1, blocking collectives, local(): back = lax.all_to_all(back, 'dp', split_axis=0, concat_axis=0, tiled=True)  11.7 us
    ppermute x13, waiting for transfers between devices, exchange(): return lax.ppermute(array, axis, [(i, i ^ k) for i in range(size)])  7.58 us
  transfers between devices with their start and end apart: 13, of which 2 were waited for; matrix products, arithmetic and copies ran while one was open for 0% of the time, Pallas kernels for 20%

profile of v3, /device:TPU:0, one launch (start us, length us, event | category | flops | bytes accessed | tf_op | source)
XLA Modules:
  0.0 53.6 jit_solution(10105841481404476570)
XLA Ops:
  0.0 0.0 copy-start.1
  0.0 1.2 %shard_map.74 = (bf16[288,128]{1,0:T(8,128)(2,1)S(1)}, bf16[288,128]{1,0:T(8,128)(2,1)S(1)}, bf16[288,128]{1,0:T(8,128)(2,1)S(1)}, bf16[288,128]{1,0:T(8,128)(2,...) custom-call(s32[8]{0:T(128)} %bitcast.12, ...), custom_call_target="tpu_custom_call" | custom-call | tf_op jit(solution)/shard_map/pallas_call | solution.py:281
  1.2 4.1 %collective-permute-start.6 = (bf16[288,128]{1,0:T(8,128)(2,1)S(1)}, bf16[288,128]{1,0:T(8,128)(2,1)S(1)}, u32[]{:S(2)}, u32[]{:S(2)}) collective-permute-start(bf16[288,128]{1,0:T(8,128)(2,1)S(1)} %get-tuple-element.36), channel_id=1, source_target_pairs={{0,16},{4,20},{8,24},{12,28},{16,0},{20,4},{24,8},{28,12},{1,17},{... | collective-permute-start | bytes 221192 | tf_op jit(solution)/shard_map/ppermute | solution.py:276
  5.3 1.3 %collective-permute-start.7 = (bf16[288,128]{1,0:T(8,128)(2,1)S(1)}, bf16[288,128]{1,0:T(8,128)(2,1)S(1)}, u32[]{:S(2)}, u32[]{:S(2)}) collective-permute-start(bf16[288,128]{1,0:T(8,128)(2,1)S(1)} %get-tuple-element.37), channel_id=1, source_target_pairs={{0,20},{4,16},{8,28},{12,24},{16,4},{20,0},{24,12},{28,8},{1,21},{... | collective-permute-start | bytes 221192 | tf_op jit(solution)/shard_map/ppermute | solution.py:276
  6.6 0.2 collective-permute-start
  6.8 1.8 %collective-permute-start.1 = (bf16[288,128]{1,0:T(8,128)(2,1)S(1)}, bf16[288,128]{1,0:T(8,128)(2,1)S(1)}, u32[]{:S(2)}, u32[]{:S(2)}) collective-permute-start(bf16[288,128]{1,0:T(8,128)(2,1)S(1)} %get-tuple-element.30), channel_id=1, source_target_pairs={{0,8},{4,12},{8,0},{12,4},{16,24},{20,28},{24,16},{28,20},{1,9},{5... | collective-permute-start | bytes 221192 | tf_op jit(solution)/shard_map/ppermute | solution.py:276
  8.7 1.4 %collective-permute-start.2 = (bf16[288,128]{1,0:T(8,128)(2,1)S(1)}, bf16[288,128]{1,0:T(8,128)(2,1)S(1)}, u32[]{:S(2)}, u32[]{:S(2)}) collective-permute-start(bf16[288,128]{1,0:T(8,128)(2,1)S(1)} %get-tuple-element.31), channel_id=1, source_target_pairs={{0,12},{4,8},{8,4},{12,0},{16,28},{20,24},{24,20},{28,16},{1,13},{... | collective-permute-start | bytes 221192 | tf_op jit(solution)/shard_map/ppermute | solution.py:276
  10.1 0.0 collective-permute-done.6.refs_0_
  10.1 4.5 %collective-permute-start.8 = (bf16[288,128]{1,0:T(8,128)(2,1)S(1)}, bf16[288,128]{1,0:T(8,128)(2,1)S(1)}, u32[]{:S(2)}, u32[]{:S(2)}) collective-permute-start(bf16[288,128]{1,0:T(8,128)(2,1)S(1)} %get-tuple-element.38), channel_id=1, source_target_pairs={{0,24},{4,28},{8,16},{12,20},{16,8},{20,12},{24,0},{28,4},{1,25},{... | collective-permute-start | bytes 221192 | tf_op jit(solution)/shard_map/ppermute | solution.py:276
  14.6 0.0 collective-permute-done.7.refs_1_
  14.6 2.4 %collective-permute-start.9 = (bf16[288,128]{1,0:T(8,128)(2,1)S(1)}, bf16[288,128]{1,0:T(8,128)(2,1)S(1)}, u32[]{:S(2)}, u32[]{:S(2)}) collective-permute-start(bf16[288,128]{1,0:T(8,128)(2,1)S(1)} %get-tuple-element.39), channel_id=1, source_target_pairs={{0,28},{4,24},{8,20},{12,16},{16,12},{20,8},{24,4},{28,0},{1,29},{... | collective-permute-start | bytes 221192 | tf_op jit(solution)/shard_map/ppermute | solution.py:276
  17.0 4.3 %shard_map.73 = (bf16[8,576,1024]{2,1,0:T(8,128)(2,1)S(1)}, f32[4,512,128]{2,1,0:T(8,128)S(1)}, f32[64,128]{1,0:T(8,128)S(1)}) custom-call(s32[8]{0:T(128)} %bitcast.13, s32[4]{0:T(128)} %bitcast.14, s32[8]{0:T(128)} %bitcast.7, bf16[4,64,576]{2,1,0:T(8,128)(2,1)} %query_hbm.3, bf16[4,576,256]{2,1,0:T(8,128)(2,1)} %bitcast.11, bf16[8,576,1024]{2,1,0:T(8,128)(2,1)} %bitcast.10), custom_call_target="tpu_custom_call" | custom-call | flops 1140850688 | bytes 9437184 | tf_op jit(solution)/shard_map/pallas_call | solution.py:281
  21.3 0.0 collective-permute-done.8.refs_2_
  21.3 0.3 collective-permute-done.9.refs_3_
  21.7 0.0 copy-done.1
  21.7 0.0 copy-start
  21.7 3.5 %shard_map.76 = (bf16[272,128]{1,0:T(8,128)(2,1)S(1)}, bf16[272,128]{1,0:T(8,128)(2,1)S(1)}, bf16[272,128]{1,0:T(8,128)(2,1)S(1)}, bf16[272,128]{1,0:T(8,128)(2,1)S(1)}) custom-call(s32[8]{0:T(128)S(1)} %bitcast.8, bf16[8,576,1024]{2,1,0:T(8,128)(2,1)S(1)} %get-tuple-element.26.host_ref, bf16[288,128]{1,0:T(8,128)(2,1)S(1)} %collective-permute-done.6.refs_0_, ...), custom_call_target="tpu_custom_call" | custom-call | flops 570425344 | bytes 4718592 | tf_op jit(solution)/shard_map/pallas_call | solution.py:281
  25.1 0.1 collective-permute-start.10
  25.2 0.0 collective-permute-done.refs_0_
  25.2 0.0 collective-permute-done.1.refs_1_
  25.2 0.0 collective-permute-done.2.refs_2_
  25.2 2.9 %shard_map.75 = (bf16[528,128]{1,0:T(8,128)(2,1)S(1)}, bf16[528,128]{1,0:T(8,128)(2,1)S(1)}, bf16[528,128]{1,0:T(8,128)(2,1)S(1)}, bf16[528,128]{1,0:T(8,128)(2,1)S(1)}) custom-call(s32[8]{0:T(128)S(1)} %bitcast.9, bf16[8,576,1024]{2,1,0:T(8,128)(2,1)S(1)} %get-tuple-element.26.host_ref, f32[4,512,128]{2,1,0:T(8,128)S(1)} %get-tuple-element.27.own_stage, ...), custom_call_target="tpu_custom_call" | custom-call | flops 427819008 | bytes 3538944 | tf_op jit(solution)/shard_map/pallas_call | solution.py:281
  28.2 0.5 %collective-permute-start.3 = (bf16[528,128]{1,0:T(8,128)(2,1)S(1)}, bf16[528,128]{1,0:T(8,128)(2,1)S(1)}, u32[]{:S(2)}, u32[]{:S(2)}) collective-permute-start(bf16[528,128]{1,0:T(8,128)(2,1)S(1)} %get-tuple-element.33), channel_id=1, source_target_pairs={{0,1},{1,0},{2,3},{3,2},{4,5},{5,4},{6,7},{7,6},{8,9},{9,8},{10,11... | collective-permute-start | bytes 405512 | tf_op jit(solution)/shard_map/ppermute | solution.py:276
  28.7 1.5 %collective-permute-start.4 = (bf16[528,128]{1,0:T(8,128)(2,1)S(1)}, bf16[528,128]{1,0:T(8,128)(2,1)S(1)}, u32[]{:S(2)}, u32[]{:S(2)}) collective-permute-start(bf16[528,128]{1,0:T(8,128)(2,1)S(1)} %get-tuple-element.34), channel_id=1, source_target_pairs={{0,2},{1,3},{2,0},{3,1},{4,6},{5,7},{6,4},{7,5},{8,10},{9,11},{10,... | collective-permute-start | bytes 405512 | tf_op jit(solution)/shard_map/ppermute | solution.py:276
  30.2 0.0 collective-permute-start.5
  30.2 1.4 %collective-permute-start.11 = (bf16[272,128]{1,0:T(8,128)(2,1)S(1)}, bf16[272,128]{1,0:T(8,128)(2,1)S(1)}, u32[]{:S(2)}, u32[]{:S(2)}) collective-permute-start(bf16[272,128]{1,0:T(8,128)(2,1)S(1)} %get-tuple-element.42), channel_id=1, source_target_pairs={{0,2},{1,3},{2,0},{3,1},{4,6},{5,7},{6,4},{7,5},{8,10},{9,11},{10,... | collective-permute-start | bytes 208904 | tf_op jit(solution)/shard_map/ppermute | solution.py:276
  31.7 0.0 collective-permute-done.10.refs_5_
  31.7 0.6 %collective-permute-start.12 = (bf16[272,128]{1,0:T(8,128)(2,1)S(1)}, bf16[272,128]{1,0:T(8,128)(2,1)S(1)}, u32[]{:S(2)}, u32[]{:S(2)}) collective-permute-start(bf16[272,128]{1,0:T(8,128)(2,1)S(1)} %get-tuple-element.43), channel_id=1, source_target_pairs={{0,3},{1,2},{2,1},{3,0},{4,7},{5,6},{6,5},{7,4},{8,11},{9,10},{10,... | collective-permute-start | bytes 208904 | tf_op jit(solution)/shard_map/ppermute | solution.py:276
  32.2 7.2 %collective-permute-done.11.refs_6_ = bf16[272,128]{1,0:T(8,128)(2,1)S(1)} collective-permute-done((bf16[272,128]{1,0:T(8,128)(2,1)S(1)}, bf16[272,128]{1,0:T(8,128)(2,1)S(1)}, u32[]{:S(2)}, u32[]{:S(2)}) %collective-permute-start.11) | collective-permute-done | bytes 69664 | tf_op jit(solution)/shard_map/ppermute | solution.py:276
  39.4 0.0 collective-permute-done.12.refs_7_
  39.4 0.0 collective-permute-done.3.refs_1_
  39.4 0.0 collective-permute-done.4.refs_2_
  39.4 0.0 collective-permute-done.5.refs_3_
  39.4 0.0 copy-done
  39.4 0.7 %shard_map.77 = (bf16[8,80,128]{2,1,0:T(8,128)(2,1)S(1)}, f32[256,128]{1,0:T(8,128)S(1)}, f32[4,16,128]{2,1,0:T(8,128)S(1)}) custom-call(bf16[16,512,128]{2,1,0:T(8,128)(2,1)S(1)} %copy-done, bf16[528,128]{1,0:T(8,128)(2,1)S(1)} %get-tuple-element.32.refs_0_, bf16[528,128]{1,0:T(8,128)(2,1)S(1)} %collective-permute-done.3.refs_1_, ...), custom_call_target="tpu_custom_call" | custom-call | tf_op jit(solution)/shard_map/pallas_call | solution.py:281
  40.2 11.7 %all_to_all.5.back_ref = bf16[8,80,128]{2,1,0:T(8,128)(2,1)S(1)} all-to-all(bf16[8,80,128]{2,1,0:T(8,128)(2,1)S(1)} %get-tuple-element.44), channel_id=1, replica_groups=mesh['dp'=8,'sub'=4] {'dp'}, dimensions={0} | all-to-all | bytes 327680 | tf_op jit(solution)/shard_map/all_to_all | solution.py:409
  51.9 1.7 %shard_map.78 = bf16[4,16,128]{2,1,0:T(8,128)(2,1)} custom-call(bf16[8,80,128]{2,1,0:T(8,128)(2,1)S(1)} %all_to_all.5.back_ref, f32[256,128]{1,0:T(8,128)S(1)} %get-tuple-element.45.own_ref, f32[4,16,128]{2,1,0:T(8,128)S(1)} %get-tuple-element.46.side_ref), custom_call_target="tpu_custom_call" | custom-call | tf_op jit(solution)/shard_map/pallas_call | solution.py:281
Async XLA Ops:
  0.0 21.7 %copy-start.1 = (s32[1,1,8]{2,1,0:T(1,128)S(1)}, s32[1,1,8]{2,1,0:T(1,128)}, u32[]{:S(2)}) copy-start(s32[1,1,8]{2,1,0:T(1,128)} %param.11) | copy-start | bytes 100
  1.2 8.9 %collective-permute-start.6 = (bf16[288,128]{1,0:T(8,128)(2,1)S(1)}, bf16[288,128]{1,0:T(8,128)(2,1)S(1)}, u32[]{:S(2)}, u32[]{:S(2)}) collective-permute-start(bf16[288,128]{1,0:T(8,128)(2,1)S(1)} %get-tuple-element.36), channel_id=1, source_target_pairs={{0,16},{4,20},{8,24},{12,28},{16,0},{20,4},{24,8},{28,12},{1,17},{... | collective-permute-start | bytes 221192 | tf_op jit(solution)/shard_map/ppermute | solution.py:276
  5.3 9.3 %collective-permute-start.7 = (bf16[288,128]{1,0:T(8,128)(2,1)S(1)}, bf16[288,128]{1,0:T(8,128)(2,1)S(1)}, u32[]{:S(2)}, u32[]{:S(2)}) collective-permute-start(bf16[288,128]{1,0:T(8,128)(2,1)S(1)} %get-tuple-element.37), channel_id=1, source_target_pairs={{0,20},{4,16},{8,28},{12,24},{16,4},{20,0},{24,12},{28,8},{1,21},{... | collective-permute-start | bytes 221192 | tf_op jit(solution)/shard_map/ppermute | solution.py:276
  6.6 18.6 %collective-permute-start = (bf16[288,128]{1,0:T(8,128)(2,1)S(1)}, bf16[288,128]{1,0:T(8,128)(2,1)S(1)}, u32[]{:S(2)}, u32[]{:S(2)}) collective-permute-start(bf16[288,128]{1,0:T(8,128)(2,1)S(1)} %get-tuple-element.29), channel_id=1, source_target_pairs={{0,4},{4,0},{8,12},{12,8},{16,20},{20,16},{24,28},{28,24},{1,5},{5... | collective-permute-start | bytes 221192 | tf_op jit(solution)/shard_map/ppermute | solution.py:276
  6.8 18.4 %collective-permute-start.1 = (bf16[288,128]{1,0:T(8,128)(2,1)S(1)}, bf16[288,128]{1,0:T(8,128)(2,1)S(1)}, u32[]{:S(2)}, u32[]{:S(2)}) collective-permute-start(bf16[288,128]{1,0:T(8,128)(2,1)S(1)} %get-tuple-element.30), channel_id=1, source_target_pairs={{0,8},{4,12},{8,0},{12,4},{16,24},{20,28},{24,16},{28,20},{1,9},{5... | collective-permute-start | bytes 221192 | tf_op jit(solution)/shard_map/ppermute | solution.py:276
  8.7 16.6 %collective-permute-start.2 = (bf16[288,128]{1,0:T(8,128)(2,1)S(1)}, bf16[288,128]{1,0:T(8,128)(2,1)S(1)}, u32[]{:S(2)}, u32[]{:S(2)}) collective-permute-start(bf16[288,128]{1,0:T(8,128)(2,1)S(1)} %get-tuple-element.31), channel_id=1, source_target_pairs={{0,12},{4,8},{8,4},{12,0},{16,28},{20,24},{24,20},{28,16},{1,13},{... | collective-permute-start | bytes 221192 | tf_op jit(solution)/shard_map/ppermute | solution.py:276
  10.1 11.2 %collective-permute-start.8 = (bf16[288,128]{1,0:T(8,128)(2,1)S(1)}, bf16[288,128]{1,0:T(8,128)(2,1)S(1)}, u32[]{:S(2)}, u32[]{:S(2)}) collective-permute-start(bf16[288,128]{1,0:T(8,128)(2,1)S(1)} %get-tuple-element.38), channel_id=1, source_target_pairs={{0,24},{4,28},{8,16},{12,20},{16,8},{20,12},{24,0},{28,4},{1,25},{... | collective-permute-start | bytes 221192 | tf_op jit(solution)/shard_map/ppermute | solution.py:276
  14.6 7.1 %collective-permute-start.9 = (bf16[288,128]{1,0:T(8,128)(2,1)S(1)}, bf16[288,128]{1,0:T(8,128)(2,1)S(1)}, u32[]{:S(2)}, u32[]{:S(2)}) collective-permute-start(bf16[288,128]{1,0:T(8,128)(2,1)S(1)} %get-tuple-element.39), channel_id=1, source_target_pairs={{0,28},{4,24},{8,20},{12,16},{16,12},{20,8},{24,4},{28,0},{1,29},{... | collective-permute-start | bytes 221192 | tf_op jit(solution)/shard_map/ppermute | solution.py:276
  21.7 17.8 %copy-start = (bf16[16,512,128]{2,1,0:T(8,128)(2,1)S(1)}, bf16[16,512,128]{2,1,0:T(8,128)(2,1)}, u32[]{:S(2)}) copy-start(bf16[16,512,128]{2,1,0:T(8,128)(2,1)} %value_ref.1) | copy-start | bytes 6291460
  25.1 6.5 %collective-permute-start.10 = (bf16[272,128]{1,0:T(8,128)(2,1)S(1)}, bf16[272,128]{1,0:T(8,128)(2,1)S(1)}, u32[]{:S(2)}, u32[]{:S(2)}) collective-permute-start(bf16[272,128]{1,0:T(8,128)(2,1)S(1)} %get-tuple-element.41), channel_id=1, source_target_pairs={{0,1},{1,0},{2,3},{3,2},{4,5},{5,4},{6,7},{7,6},{8,9},{9,8},{10,11... | collective-permute-start | bytes 208904 | tf_op jit(solution)/shard_map/ppermute | solution.py:276
  28.2 11.2 %collective-permute-start.3 = (bf16[528,128]{1,0:T(8,128)(2,1)S(1)}, bf16[528,128]{1,0:T(8,128)(2,1)S(1)}, u32[]{:S(2)}, u32[]{:S(2)}) collective-permute-start(bf16[528,128]{1,0:T(8,128)(2,1)S(1)} %get-tuple-element.33), channel_id=1, source_target_pairs={{0,1},{1,0},{2,3},{3,2},{4,5},{5,4},{6,7},{7,6},{8,9},{9,8},{10,11... | collective-permute-start | bytes 405512 | tf_op jit(solution)/shard_map/ppermute | solution.py:276
  28.7 10.7 %collective-permute-start.4 = (bf16[528,128]{1,0:T(8,128)(2,1)S(1)}, bf16[528,128]{1,0:T(8,128)(2,1)S(1)}, u32[]{:S(2)}, u32[]{:S(2)}) collective-permute-start(bf16[528,128]{1,0:T(8,128)(2,1)S(1)} %get-tuple-element.34), channel_id=1, source_target_pairs={{0,2},{1,3},{2,0},{3,1},{4,6},{5,7},{6,4},{7,5},{8,10},{9,11},{10,... | collective-permute-start | bytes 405512 | tf_op jit(solution)/shard_map/ppermute | solution.py:276
  30.2 9.2 %collective-permute-start.5 = (bf16[528,128]{1,0:T(8,128)(2,1)S(1)}, bf16[528,128]{1,0:T(8,128)(2,1)S(1)}, u32[]{:S(2)}, u32[]{:S(2)}) collective-permute-start(bf16[528,128]{1,0:T(8,128)(2,1)S(1)} %get-tuple-element.35), channel_id=1, source_target_pairs={{0,3},{1,2},{2,1},{3,0},{4,7},{5,6},{6,5},{7,4},{8,11},{9,10},{10,... | collective-permute-start | bytes 405512 | tf_op jit(solution)/shard_map/ppermute | solution.py:276
  30.2 9.2 %collective-permute-start.11 = (bf16[272,128]{1,0:T(8,128)(2,1)S(1)}, bf16[272,128]{1,0:T(8,128)(2,1)S(1)}, u32[]{:S(2)}, u32[]{:S(2)}) collective-permute-start(bf16[272,128]{1,0:T(8,128)(2,1)S(1)} %get-tuple-element.42), channel_id=1, source_target_pairs={{0,2},{1,3},{2,0},{3,1},{4,6},{5,7},{6,4},{7,5},{8,10},{9,11},{10,... | collective-permute-start | bytes 208904 | tf_op jit(solution)/shard_map/ppermute | solution.py:276
  31.7 7.8 %collective-permute-start.12 = (bf16[272,128]{1,0:T(8,128)(2,1)S(1)}, bf16[272,128]{1,0:T(8,128)(2,1)S(1)}, u32[]{:S(2)}, u32[]{:S(2)}) collective-permute-start(bf16[272,128]{1,0:T(8,128)(2,1)S(1)} %get-tuple-element.43), channel_id=1, source_target_pairs={{0,3},{1,2},{2,1},{3,0},{4,7},{5,6},{6,5},{7,4},{8,11},{9,10},{10,... | collective-permute-start | bytes 208904 | tf_op jit(solution)/shard_map/ppermute | solution.py:276
